TPU v7x, 128 devices: a whole 4x4x4 slice. The times are simulated.
128 devices in a mesh: shards: 16 (over x, y), tensor: 4 (over z), section: 2 (over core).
Axes of the slice: x: 4, y: 4, z: 4, core: 2. Of those that a mesh axis runs over, the one named last changes fastest.
Arguments:
- gradient: bfloat16 [4, 768, 2048], P('section', 'tensor', 'shards'), may hold values from -36 to 36, as said below
- weight: bfloat16 [4, 768, 2048], P('section', 'tensor', 'shards'), may hold values from -0.21875 to 0.21875
- projector: float32 [4, 768, 256], P('section', 'tensor'), may hold values from -0.21875 to 0.21875
- first_moment: float32 [4, 256, 2048], P('section', 'tensor', 'shards'), may hold values from -0.3125 to 0.3125
- squared_moment: float32 [4, 256, 2048], P('section', 'tensor', 'shards'), may hold values from 1e-07 to 1e-05
- step_count: int32 [4], P('section'), may hold values from 1 to 11
- norm_gains: float32 [4, 768], P('section', 'tensor'), may hold values from 0.5 to 1.5
- gain_gradient: float32 [4, 768], P('section', 'tensor'), may hold values from -0.15625 to 0.15625
- gain_first: float32 [4, 768], P('section', 'tensor'), may hold values from -0.046875 to 0.046875
- gain_second: float32 [4, 768], P('section', 'tensor'), may hold values from 1e-08 to 1e-06
Outputs:
- weight_next: bfloat16 [4, 768, 2048], P('section', 'tensor', 'shards')
- fresh_projector: float32 [4, 768, 256], P('section', 'tensor')
- new_first: float32 [4, 256, 2048], P('section', 'tensor', 'shards')
- new_second: float32 [4, 256, 2048], P('section', 'tensor', 'shards')
- new_gains: float32 [4, 768], P('section', 'tensor')
- new_gain_first: float32 [4, 768], P('section', 'tensor')
- new_gain_second: float32 [4, 768], P('section', 'tensor')
Inputs may be any that keep to these rules, and one draw needn't show every extreme that they name: `gradient`: gradient entries are finite real numbers.
All inputs are finite; a program needn't handle non-finite values.
Results may differ from a plain program's by a relative error of at most 0.001.
Values sent between devices are 32-bit elements; how exact they have to be, the bound alone decides.
No kernel may reach another device: no remote copies, remote signals or barrier semaphores. Data moves between devices by JAX's collectives and lax.ppermute only.
A program may use at most 64 MiB of HBM per device.

v0:
```python
import jax
import jax.numpy as jnp
from jax import lax
from jax.experimental import pallas as pl
from jax.experimental.pallas import tpu as pltpu
from jax.sharding import PartitionSpec as P


NS_STEPS = 5
BETA_ONE = 0.9
BETA_TWO = 0.999
EPSILON = 1e-08
NORM_EPS = 1e-06
LEARN_RATE = 0.01
GALORE_SCALE = 0.25
WEIGHT_DECAY = 0.1


F32 = jnp.float32
BF16 = jnp.bfloat16
TENSOR = 4
VMEM = pl.BlockSpec(memory_space=pltpu.VMEM)
SMEM = pl.BlockSpec(memory_space=pltpu.SMEM)


def split(x):
    hi = x.astype(BF16)
    return hi, (x - hi.astype(F32)).astype(BF16)


def dot(a, b, dims=((1,), (0,))):
    return lax.dot_general(a, b, (dims, ((), ())), preferred_element_type=F32)


def dot3(a, b, dims=((1,), (0,))):
    return dot(a[0], b[0], dims) + (dot(a[0], b[1], dims) + dot(a[1], b[0], dims))


def dot_exact_left(a, b, dims=((1,), (0,))):
    return dot(a, b[0], dims) + dot(a, b[1], dims)


def fold_kernel(gradient, projector, own, s1, s2, s3):
    _, rows, _ = gradient.shape
    half = own.shape[1]
    me = lax.axis_index("tensor")
    for k, out in enumerate((own, s1, s2, s3)):
        peer = lax.rem(me + k, TENSOR)
        m, h = peer // 2, lax.rem(peer, 2)
        g = gradient[m]
        p = projector[m, :, pl.ds(pl.multiple_of(h * half, half), half)]
        f = dot_exact_left(g, split(p), ((0,), (0,)))
        if k == 0:
            out[...] = f
        else:
            out[:rows] = g.astype(F32)
            out[rows:] = f


def pack_kernel(gradient, first, second, p1, p2, p3):
    mats, rows, _ = gradient.shape
    own_rank = first.shape[1]
    me = lax.axis_index("tensor")
    for k, out in enumerate((p1, p2, p3)):
        m = lax.rem(me + k + 1, TENSOR) // 2
        out[:rows] = gradient[1 - m].astype(F32)
        for i in range(mats):
            out[rows + i * own_rank : rows + (i + 1) * own_rank] = first[i]
            at = rows + (mats + i) * own_rank
            out[at : at + own_rank] = second[i]


def range_kernel(gradient, own, r1, r2, r3, ranged):
    _, rows, _ = gradient.shape
    me = lax.axis_index("tensor")
    total = (own[...] + r1[rows:]) + (r2[rows:] + r3[rows:])
    total = split(total)
    for k, r in enumerate((None, r1, r2, r3)):
        peer = lax.rem(me + (TENSOR - k), TENSOR)
        g = gradient[me // 2] if k == 0 else r[:rows].astype(BF16)
        ranged[pl.ds(pl.multiple_of(peer * rows, 8), rows), :] = dot_exact_left(g, total)


def spread_kernel(parts, out):
    total = jnp.sum(parts[...], axis=0)
    for i in range(out.shape[0]):
        out[i] = total


def finish_kernel(
    ranged, gradient, first, second, r1, r2, r3, p1, p2, p3, weight, corrections,
    weight_next, fresh, new_first, new_second,
    projected_at, direction_at,
):
    mats, rows, cols = gradient.shape
    own_rank = first.shape[1]
    half = ranged.shape[2]
    rank = 2 * half
    me = lax.axis_index("tensor")
    eye = (
        lax.broadcasted_iota(jnp.int32, (rank, rank), 0)
        == lax.broadcasted_iota(jnp.int32, (rank, rank), 1)
    ).astype(F32)
    owner = [lax.rem(me + (TENSOR - k), TENSOR) for k in range(TENSOR)]
    which = (me // 2, 1 - me // 2)
    sides = ((None, r1, r2, r3), (None, p1, p2, p3))
    moments = (None, p1, p2, p3)
    state = []
    for m, side in zip(which, sides):
        gram = jnp.zeros((rank, rank), F32)
        cross = jnp.zeros((rank, cols), F32)
        squares = jnp.zeros((8, rank), F32)
        for k in range(TENSOR):
            at = pl.ds(pl.multiple_of(owner[k] * rows, 8), rows)
            y = jnp.concatenate([ranged[2 * m, at, :], ranged[2 * m + 1, at, :]], axis=1)
            ys = split(y)
            yt = (ys[0].T, ys[1].T)
            g = gradient[m] if k == 0 else side[k][:rows].astype(BF16)
            gram += dot3(yt, ys)
            cross += dot(yt[0], g) + dot(yt[1], g)
            squares += jnp.sum((y * y).reshape(rows // 8, 8, rank), axis=0)
            if k == 0:
                mine = y
        inverse = 1.0 / (jnp.sqrt(jnp.sum(squares)) + NORM_EPS)
        state.append([gram * (inverse * inverse), cross * inverse, mine * inverse])
    for sweep in range(NS_STEPS):
        for i in range(mats):
            gram, cross, mine = state[i]
            step = split(1.5 * eye - 0.5 * gram)
            cross = dot3(step, split(cross))
            mine = dot3(split(mine), step)
            if sweep < NS_STEPS - 1:
                gram = dot3(split(dot3(step, split(gram))), step)
            state[i] = [gram, cross, mine]
    for i, m in enumerate(which):
        _, cross, mine = state[i]
        fresh[m] = mine
        projected_at[i] = cross
        c1 = corrections[m, 0]
        c2 = corrections[m, 1]
        for k in range(TENSOR):
            at = pl.ds(pl.multiple_of(owner[k] * own_rank, 8), own_rank)
            projected = projected_at[i, at, :]
            if k == 0:
                m1, m2 = first[m], second[m]
            else:
                from_first = pl.multiple_of(rows + m * own_rank, 8)
                from_second = pl.multiple_of(rows + (mats + m) * own_rank, 8)
                m1 = moments[k][pl.ds(from_first, own_rank), :]
                m2 = moments[k][pl.ds(from_second, own_rank), :]
            n1 = BETA_ONE * m1 + (1.0 - BETA_ONE) * projected
            n2 = BETA_TWO * m2 + (1.0 - BETA_TWO) * projected * projected
            if k == 0:
                new_first[m] = n1
                new_second[m] = n2
            direction_at[i, at, :] = n1 / c1 / (jnp.sqrt(n2 / c2) + EPSILON)
        update = dot3(split(mine), split(direction_at[i]))
        w = weight[m].astype(F32)
        weight_next[m] = (
            w - LEARN_RATE * (GALORE_SCALE * update + WEIGHT_DECAY * w)
        ).astype(BF16)


def shards(
    gradient,
    weight,
    projector,
    first_moment,
    squared_moment,
    step_count,
    norm_gains,
    gain_gradient,
    gain_first,
    gain_second,
):
    mats, rows, cols = gradient.shape
    rank = projector.shape[2]
    own_rank = first_moment.shape[1]
    half = rank // 2
    spread = lax.axis_size("shards")
    block = TENSOR * rows // spread
    shape = jax.ShapeDtypeStruct

    def shifted(x, k):
        return lax.ppermute(x, "tensor", [(i, (i + k) % TENSOR) for i in range(TENSOR)])

    def call(kernel, out_shape, inputs, mib, in_specs=None, **more):
        outs = out_shape if isinstance(out_shape, tuple) else (out_shape,)
        got = pl.pallas_call(
            kernel,
            out_shape=outs,
            in_specs=in_specs or [VMEM] * len(inputs),
            out_specs=(VMEM,) * len(outs),
            compiler_params=pltpu.CompilerParams(vmem_limit_bytes=mib << 20),
            **more,
        )(*inputs)
        return got if isinstance(out_shape, tuple) else got[0]

    own, s1, s2, s3 = call(
        fold_kernel,
        (shape((cols, half), F32),) + (shape((rows + cols, half), F32),) * 3,
        (gradient, projector),
        8,
    )
    r2, r3, r1 = shifted(s2, 2), shifted(s3, 3), shifted(s1, 1)
    p1, p2, p3 = call(
        pack_kernel,
        (shape((rows + 2 * mats * own_rank, cols), F32),) * 3,
        (gradient, first_moment, squared_moment),
        8,
    )
    q2, q3, q1 = shifted(p2, 2), shifted(p3, 3), shifted(p1, 1)

    steps = step_count.astype(F32)[:, None]
    correct_one = 1.0 - BETA_ONE**steps
    correct_two = 1.0 - BETA_TWO**steps
    new_gain_first = BETA_ONE * gain_first + (1.0 - BETA_ONE) * gain_gradient
    new_gain_second = BETA_TWO * gain_second + (1.0 - BETA_TWO) * gain_gradient * gain_gradient
    new_gains = norm_gains - LEARN_RATE * (new_gain_first / correct_one) / (
        jnp.sqrt(new_gain_second / correct_two) + EPSILON
    )
    corrections = jnp.concatenate([correct_one, correct_two], axis=1)

    ranged_part = call(
        range_kernel, shape((TENSOR * rows, half), F32), (gradient, own, r1, r2, r3), 8
    )
    parts = lax.all_to_all(ranged_part, "shards", 0, 0, tiled=True)
    blocks = call(
        spread_kernel,
        shape((spread * TENSOR, block, half), F32),
        (parts.reshape(spread, block, half),),
        8,
    )
    ranged = lax.all_to_all(
        blocks.reshape(spread * TENSOR * block, half), ("tensor", "shards"), 0, 0, tiled=True
    ).reshape(TENSOR, spread * block, half)
    weight_next, fresh_projector, new_first, new_second = call(
        finish_kernel,
        (
            shape(weight.shape, weight.dtype),
            shape(projector.shape, F32),
            shape(first_moment.shape, F32),
            shape(squared_moment.shape, F32),
        ),
        (
            ranged, gradient, first_moment, squared_moment,
            r1, r2, r3, q1, q2, q3, weight, corrections,
        ),
        32,
        in_specs=[VMEM] * 11 + [SMEM],
        scratch_shapes=[pltpu.VMEM((mats, rank, cols), F32), pltpu.VMEM((mats, rank, cols), F32)],
    )
    return (
        weight_next,
        fresh_projector,
        new_first,
        new_second,
        new_gains,
        new_gain_first,
        new_gain_second,
    )


def solution(mesh):
    return jax.shard_map(
        shards,
        mesh=mesh,
        in_specs=(
            P("section", "tensor", "shards"),
            P("section", "tensor", "shards"),
            P("section", "tensor", None),
            P("section", "tensor", "shards"),
            P("section", "tensor", "shards"),
            P("section"),
            P("section", "tensor"),
            P("section", "tensor"),
            P("section", "tensor"),
            P("section", "tensor"),
        ),
        out_specs=(
            P("section", "tensor", "shards"),
            P("section", "tensor", None),
            P("section", "tensor", "shards"),
            P("section", "tensor", "shards"),
            P("section", "tensor"),
            P("section", "tensor"),
            P("section", "tensor"),
        ),
        check_vma=False,
    )
```

profile of v0, /device:TPU:0, one launch (start us, length us, event | category | flops | bytes accessed | tf_op | source)
XLA Modules:
  0.0 78.5 jit_solution(11435094133357317185)
XLA Ops:
  0.6 0.0 copy-start
  0.6 0.9 %copy-done = bf16[2,192,128]{2,1,0:T(8,128)(2,1)S(1)} copy-done((bf16[2,192,128]{2,1,0:T(8,128)(2,1)S(1)}, bf16[2,192,128]{2,1,0:T(8,128)(2,1)}, u32[]{:S(2)}) %copy-start) | copy-done | bytes 98328
  1.5 0.0 copy-start.2
  1.5 1.0 %copy-done.2 = f32[2,192,256]{2,1,0:T(8,128)S(1)} copy-done((f32[2,192,256]{2,1,0:T(8,128)S(1)}, f32[2,192,256]{2,1,0:T(8,128)}, u32[]{:S(2)}) %copy-start.2) | copy-done | bytes 393240
  2.5 0.4 shard_map.153
  2.9 2.1 %collective-permute-start = (f32[320,128]{1,0:T(8,128)S(1)}, f32[320,128]{1,0:T(8,128)S(1)}, u32[]{:S(2)}, u32[]{:S(2)}) collective-permute-start(f32[320,128]{1,0:T(8,128)S(1)} %get-tuple-element.19), channel_id=1, source_target_pairs={{0,2},{2,4},{4,6},{6,0},{1,3},{3,5},{5,7},{7,1},{8,10},{10,12},{12... | collective-permute-start | bytes 491528 | tf_op jit(solution)/shard_map/ppermute | solution.py:185
  5.0 3.6 %collective-permute-start.1 = (f32[320,128]{1,0:T(8,128)S(1)}, f32[320,128]{1,0:T(8,128)S(1)}, u32[]{:S(2)}, u32[]{:S(2)}) collective-permute-start(f32[320,128]{1,0:T(8,128)S(1)} %get-tuple-element.20), channel_id=1, source_target_pairs={{0,4},{2,6},{4,0},{6,2},{1,5},{3,7},{5,1},{7,3},{8,12},{10,14},{12... | collective-permute-start | bytes 491528 | tf_op jit(solution)/shard_map/ppermute | solution.py:185
  8.6 1.0 %collective-permute-start.2 = (f32[320,128]{1,0:T(8,128)S(1)}, f32[320,128]{1,0:T(8,128)S(1)}, u32[]{:S(2)}, u32[]{:S(2)}) collective-permute-start(f32[320,128]{1,0:T(8,128)S(1)} %get-tuple-element.21), channel_id=1, source_target_pairs={{0,6},{2,0},{4,2},{6,4},{1,7},{3,1},{5,3},{7,5},{8,14},{10,8},{12,... | collective-permute-start | bytes 491528 | tf_op jit(solution)/shard_map/ppermute | solution.py:185
  9.6 1.7 %collective-permute-done.r1 = f32[320,128]{1,0:T(8,128)S(1)} collective-permute-done((f32[320,128]{1,0:T(8,128)S(1)}, f32[320,128]{1,0:T(8,128)S(1)}, u32[]{:S(2)}, u32[]{:S(2)}) %collective-permute-start) | collective-permute-done | bytes 163872 | tf_op jit(solution)/shard_map/ppermute | solution.py:185
  11.3 4.7 %collective-permute-done.1.r2 = f32[320,128]{1,0:T(8,128)S(1)} collective-permute-done((f32[320,128]{1,0:T(8,128)S(1)}, f32[320,128]{1,0:T(8,128)S(1)}, u32[]{:S(2)}, u32[]{:S(2)}) %collective-permute-start.1) | collective-permute-done | bytes 163872 | tf_op jit(solution)/shard_map/ppermute | solution.py:185
  16.0 0.0 collective-permute-done.2.r3
  16.0 0.3 shard_map.154
  16.3 16.0 %all_to_all.15.parts = f32[16,48,128]{2,1,0:T(8,128)S(1)} all-to-all(f32[16,48,128]{2,1,0:T(8,128)S(1)} %bitcast.7), channel_id=1, replica_groups=mesh['shards'=16,'tensor'=4,'section'=2] {'shards'}, dimensions={0} | all-to-all | bytes 786432 | tf_op jit(solution)/shard_map/all_to_all | solution.py:227
  32.2 1.3 %shard_map.155 = f32[64,48,128]{2,1,0:T(8,128)} custom-call(f32[16,48,128]{2,1,0:T(8,128)S(1)} %all_to_all.15.parts), custom_call_target="tpu_custom_call" | custom-call | tf_op jit(solution)/shard_map/pallas_call | solution.py:189
  33.5 0.0 copy-start.1
  33.5 0.0 copy-start.3
  33.5 0.0 copy-start.4
  33.5 0.0 copy-start.9
  33.5 0.0 copy-start.6
  33.5 0.0 copy-start.7
  33.5 0.0 copy-start.8
  33.6 0.0 copy-start.5
  33.6 6.9 %all-to-all-start.1 = ((f32[64,48,128]{2,1,0:T(8,128)}), f32[64,48,128]{2,1,0:T(8,128)S(1)}, u32[]{:S(2)}, u32[]{:S(2)}) async-start(f32[64,48,128]{2,1,0:T(8,128)} %shard_map.155), calls=%async_computation.1 | async-start | bytes 3145728 | tf_op jit(solution)/shard_map/all_to_all | solution.py:234
  40.5 0.0 copy-done.1
  40.5 0.0 copy-done.3
  40.5 0.0 copy-done.4
  40.5 0.7 shard_map.156
  41.2 1.6 %collective-permute-start.3 = (f32[448,128]{1,0:T(8,128)}, f32[448,128]{1,0:T(8,128)S(1)}, u32[]{:S(2)}, u32[]{:S(2)}) collective-permute-start(f32[448,128]{1,0:T(8,128)} %get-tuple-element.22), channel_id=1, source_target_pairs={{0,2},{2,4},{4,6},{6,0},{1,3},{3,5},{5,7},{7,1},{8,10},{10,12},{12... | collective-permute-start | bytes 688136 | tf_op jit(solution)/shard_map/ppermute | solution.py:185
  42.8 2.9 %collective-permute-start.4 = (f32[448,128]{1,0:T(8,128)S(1)}, f32[448,128]{1,0:T(8,128)S(1)}, u32[]{:S(2)}, u32[]{:S(2)}) collective-permute-start(f32[448,128]{1,0:T(8,128)S(1)} %get-tuple-element.23), channel_id=1, source_target_pairs={{0,4},{2,6},{4,0},{6,2},{1,5},{3,7},{5,1},{7,3},{8,12},{10,14},{12... | collective-permute-start | bytes 688136 | tf_op jit(solution)/shard_map/ppermute | solution.py:185
  45.7 1.4 %collective-permute-start.5 = (f32[448,128]{1,0:T(8,128)S(1)}, f32[448,128]{1,0:T(8,128)S(1)}, u32[]{:S(2)}, u32[]{:S(2)}) collective-permute-start(f32[448,128]{1,0:T(8,128)S(1)} %get-tuple-element.24), channel_id=1, source_target_pairs={{0,6},{2,0},{4,2},{6,4},{1,7},{3,1},{5,3},{7,5},{8,14},{10,8},{12,... | collective-permute-start | bytes 688136 | tf_op jit(solution)/shard_map/ppermute | solution.py:185
  47.1 0.0 copy-done.9
  47.1 0.5 power_subtract_fusion.1
  47.6 1.3 %copy.17 = f32[2,1]{1,0:T(2,128)} copy(f32[2,1]{0,1:T(1,128)} %get-tuple-element.34) | data formatting | bytes 16 | tf_op jit(solution)/shard_map/sub | solution.py:215
  48.9 1.3 %copy.18 = f32[2,1]{1,0:T(2,128)} copy(f32[2,1]{0,1:T(1,128)} %get-tuple-element.33) | data formatting | bytes 16 | tf_op jit(solution)/shard_map/sub | solution.py:216
  50.2 0.8 pad_maximum_fusion.corrections
  51.0 0.0 copy-done.6
  51.0 0.0 copy-done.7
  51.0 0.0 copy-done.8
  51.0 1.4 %divide_subtract_fusion = (f32[2,192]{1,0:T(2,128)}, f32[2,192]{1,0:T(2,128)}, f32[2,192]{1,0:T(2,128)}) fusion(f32[2,192]{1,0:T(2,128)S(1)} %copy-done.6, f32[2]{0:T(128)} %get-tuple-element.35, f32[2]{0:T(128)} %get-tuple-element.32, f32[2,192]{1,0:T(2,128)S(1)} %copy-done.7, f32[2,192]{1,0:T(2,128)S(1)} %copy-done.8, f32[2,192]{1,0:T(2,128)} %param.19), kind=kLoop, calls=%fused_computation.2 | loop fusion | flops 4992 | bytes 10768 | tf_op jit(solution)/shard_map/sub | solution.py:219
  52.4 12.4 %collective-permute-done.3.p1 = f32[448,128]{1,0:T(8,128)S(1)} collective-permute-done((f32[448,128]{1,0:T(8,128)}, f32[448,128]{1,0:T(8,128)S(1)}, u32[]{:S(2)}, u32[]{:S(2)}) %collective-permute-start.3) | collective-permute-done | bytes 229408 | tf_op jit(solution)/shard_map/ppermute | solution.py:185
  64.8 5.9 %collective-permute-done.4.p2 = f32[448,128]{1,0:T(8,128)S(1)} collective-permute-done((f32[448,128]{1,0:T(8,128)S(1)}, f32[448,128]{1,0:T(8,128)S(1)}, u32[]{:S(2)}, u32[]{:S(2)}) %collective-permute-start.4) | collective-permute-done | bytes 229408 | tf_op jit(solution)/shard_map/ppermute | solution.py:185
  70.6 0.0 collective-permute-done.5.p3
  70.6 0.0 all-to-all-done.1
  70.6 0.0 copy-done.5
  70.6 7.9 %shard_map.157 = (bf16[2,192,128]{2,1,0:T(8,128)(2,1)}, f32[2,192,256]{2,1,0:T(8,128)}, f32[2,64,128]{2,1,0:T(8,128)}, f32[2,64,128]{2,1,0:T(8,128)}) custom-call(f32[4,768,128]{2,1,0:T(8,128)S(1)} %bitcast.6, bf16[2,192,128]{2,1,0:T(8,128)(2,1)S(1)} %copy-done.1, f32[2,64,128]{2,1,0:T(8,128)S(1)} %copy-done.3, f32[2,64,128]{2,1,0:T(8,128)S(1)} %copy-done.4, ...), custom_call_target="tpu_custom_call" | custom-call | tf_op jit(solution)/shard_map/pallas_call | solution.py:189
Async XLA Ops:
  0.6 0.9 %copy-start = (bf16[2,192,128]{2,1,0:T(8,128)(2,1)S(1)}, bf16[2,192,128]{2,1,0:T(8,128)(2,1)}, u32[]{:S(2)}) copy-start(bf16[2,192,128]{2,1,0:T(8,128)(2,1)} %gradient.7) | copy-start | bytes 294916
  1.5 1.0 %copy-start.2 = (f32[2,192,256]{2,1,0:T(8,128)S(1)}, f32[2,192,256]{2,1,0:T(8,128)}, u32[]{:S(2)}) copy-start(f32[2,192,256]{2,1,0:T(8,128)} %projector.1) | copy-start | bytes 1179652
  2.9 8.4 %collective-permute-start = (f32[320,128]{1,0:T(8,128)S(1)}, f32[320,128]{1,0:T(8,128)S(1)}, u32[]{:S(2)}, u32[]{:S(2)}) collective-permute-start(f32[320,128]{1,0:T(8,128)S(1)} %get-tuple-element.19), channel_id=1, source_target_pairs={{0,2},{2,4},{4,6},{6,0},{1,3},{3,5},{5,7},{7,1},{8,10},{10,12},{12... | collective-permute-start | bytes 491528 | tf_op jit(solution)/shard_map/ppermute | solution.py:185
  5.0 11.0 %collective-permute-start.1 = (f32[320,128]{1,0:T(8,128)S(1)}, f32[320,128]{1,0:T(8,128)S(1)}, u32[]{:S(2)}, u32[]{:S(2)}) collective-permute-start(f32[320,128]{1,0:T(8,128)S(1)} %get-tuple-element.20), channel_id=1, source_target_pairs={{0,4},{2,6},{4,0},{6,2},{1,5},{3,7},{5,1},{7,3},{8,12},{10,14},{12... | collective-permute-start | bytes 491528 | tf_op jit(solution)/shard_map/ppermute | solution.py:185
  8.6 7.4 %collective-permute-start.2 = (f32[320,128]{1,0:T(8,128)S(1)}, f32[320,128]{1,0:T(8,128)S(1)}, u32[]{:S(2)}, u32[]{:S(2)}) collective-permute-start(f32[320,128]{1,0:T(8,128)S(1)} %get-tuple-element.21), channel_id=1, source_target_pairs={{0,6},{2,0},{4,2},{6,4},{1,7},{3,1},{5,3},{7,5},{8,14},{10,8},{12,... | collective-permute-start | bytes 491528 | tf_op jit(solution)/shard_map/ppermute | solution.py:185
  33.5 7.0 %copy-start.1 = (bf16[2,192,128]{2,1,0:T(8,128)(2,1)S(1)}, bf16[2,192,128]{2,1,0:T(8,128)(2,1)}, u32[]{:S(2)}) copy-start(bf16[2,192,128]{2,1,0:T(8,128)(2,1)} %gradient.7) | copy-start | bytes 294916
  33.5 7.0 %copy-start.3 = (f32[2,64,128]{2,1,0:T(8,128)S(1)}, f32[2,64,128]{2,1,0:T(8,128)}, u32[]{:S(2)}) copy-start(f32[2,64,128]{2,1,0:T(8,128)} %first.3) | copy-start | bytes 196612
  33.5 7.0 %copy-start.4 = (f32[2,64,128]{2,1,0:T(8,128)S(1)}, f32[2,64,128]{2,1,0:T(8,128)}, u32[]{:S(2)}) copy-start(f32[2,64,128]{2,1,0:T(8,128)} %second.3) | copy-start | bytes 196612
  33.5 13.5 %copy-start.9 = (s32[2]{0:T(128)S(1)}, s32[2]{0:T(128)}, u32[]{:S(2)}) copy-start(s32[2]{0:T(128)} %param.15) | copy-start | bytes 28
  33.5 17.4 %copy-start.6 = (f32[2,192]{1,0:T(2,128)S(1)}, f32[2,192]{1,0:T(2,128)}, u32[]{:S(2)}) copy-start(f32[2,192]{1,0:T(2,128)} %param.16) | copy-start | bytes 4612
  33.5 17.4 %copy-start.7 = (f32[2,192]{1,0:T(2,128)S(1)}, f32[2,192]{1,0:T(2,128)}, u32[]{:S(2)}) copy-start(f32[2,192]{1,0:T(2,128)} %param.17) | copy-start | bytes 4612
  33.5 17.4 %copy-start.8 = (f32[2,192]{1,0:T(2,128)S(1)}, f32[2,192]{1,0:T(2,128)}, u32[]{:S(2)}) copy-start(f32[2,192]{1,0:T(2,128)} %param.18) | copy-start | bytes 4612
  33.6 37.1 %copy-start.5 = (bf16[2,192,128]{2,1,0:T(8,128)(2,1)S(1)}, bf16[2,192,128]{2,1,0:T(8,128)(2,1)}, u32[]{:S(2)}) copy-start(bf16[2,192,128]{2,1,0:T(8,128)(2,1)} %weight.1) | copy-start | bytes 294916
  33.6 37.1 %all-to-all-start.1 = ((f32[64,48,128]{2,1,0:T(8,128)}), f32[64,48,128]{2,1,0:T(8,128)S(1)}, u32[]{:S(2)}, u32[]{:S(2)}) async-start(f32[64,48,128]{2,1,0:T(8,128)} %shard_map.155), calls=%async_computation.1 | async-start | bytes 3145728 | tf_op jit(solution)/shard_map/all_to_all | solution.py:234
  41.2 23.5 %collective-permute-start.3 = (f32[448,128]{1,0:T(8,128)}, f32[448,128]{1,0:T(8,128)S(1)}, u32[]{:S(2)}, u32[]{:S(2)}) collective-permute-start(f32[448,128]{1,0:T(8,128)} %get-tuple-element.22), channel_id=1, source_target_pairs={{0,2},{2,4},{4,6},{6,0},{1,3},{3,5},{5,7},{7,1},{8,10},{10,12},{12... | collective-permute-start | bytes 688136 | tf_op jit(solution)/shard_map/ppermute | solution.py:185
  42.8 27.8 %collective-permute-start.4 = (f32[448,128]{1,0:T(8,128)S(1)}, f32[448,128]{1,0:T(8,128)S(1)}, u32[]{:S(2)}, u32[]{:S(2)}) collective-permute-start(f32[448,128]{1,0:T(8,128)S(1)} %get-tuple-element.23), channel_id=1, source_target_pairs={{0,4},{2,6},{4,0},{6,2},{1,5},{3,7},{5,1},{7,3},{8,12},{10,14},{12... | collective-permute-start | bytes 688136 | tf_op jit(solution)/shard_map/ppermute | solution.py:185
  45.7 24.9 %collective-permute-start.5 = (f32[448,128]{1,0:T(8,128)S(1)}, f32[448,128]{1,0:T(8,128)S(1)}, u32[]{:S(2)}, u32[]{:S(2)}) collective-permute-start(f32[448,128]{1,0:T(8,128)S(1)} %get-tuple-element.24), channel_id=1, source_target_pairs={{0,6},{2,0},{4,2},{6,4},{1,7},{3,1},{5,3},{7,5},{8,14},{10,8},{12,... | collective-permute-start | bytes 688136 | tf_op jit(solution)/shard_map/ppermute | solution.py:185
where the time goes:
time: 79.2 us; the launch traced here: 78.5 us
  waiting for transfers between devices  24.7 us (31%)
  starting transfers between devices  19.4 us (24%)
  blocking collectives  16 us (20%)
  Pallas kernels  10.5 us (13%)
  local copies, waits for them, and re-layouts  4.51 us (6%)
  other arithmetic  2.69 us (3%)
    ppermute x6, waiting for transfers between devices, shifted(): lax.ppermute(x, 'tensor', [(i, (i + k) % TENSOR) for i in range(TENSOR)])  24.7 us
    all_to_all x1, blocking collectives, shards(): parts = lax.all_to_all(ranged_part, 'shards', 0, 0, tiled=True)  16 us
    ppermute x6, starting transfers between devices, shifted(): lax.ppermute(x, 'tensor', [(i, (i + k) % TENSOR) for i in range(TENSOR)])  12.5 us
    pallas_call x5, Pallas kernels, call(): pl.pallas_call(kernel, out_shape=outs, in_specs=in_specs or [VMEM] * len(...  10.5 us
    all_to_all x1, starting transfers between devices, shards(): lax.all_to_all(blocks.reshape(spread * TENSOR * block, half), ('tensor',...  6.91 us
    unnamed x20, local copies, waits for them, and re-layouts  1.92 us
  transfers between devices with their start and end apart: 7, of which 4 were waited for; matrix products, arithmetic and copies ran while one was open for 7% of the time, Pallas kernels for 1%

commit v1 on v0

v1 whole, which is shorter than its diff:
```python
import functools

import jax
import jax.numpy as jnp
from jax import lax
from jax.experimental import pallas as pl
from jax.experimental.pallas import tpu as pltpu
from jax.sharding import PartitionSpec as P


NS_STEPS = 5
BETA_ONE = 0.9
BETA_TWO = 0.999
EPSILON = 1e-08
NORM_EPS = 1e-06
LEARN_RATE = 0.01
GALORE_SCALE = 0.25
WEIGHT_DECAY = 0.1


F32 = jnp.float32
BF16 = jnp.bfloat16
TENSOR = 4
VMEM = pl.BlockSpec(memory_space=pltpu.VMEM)
SMEM = pl.BlockSpec(memory_space=pltpu.SMEM)


def split(x):
    hi = x.astype(BF16)
    return hi, (x - hi.astype(F32)).astype(BF16)


def dot(a, b, dims=((1,), (0,))):
    return lax.dot_general(a, b, (dims, ((), ())), preferred_element_type=F32)


def dot3(a, b, dims=((1,), (0,))):
    return dot(a[0], b[0], dims) + (dot(a[0], b[1], dims) + dot(a[1], b[0], dims))


def dot_exact_left(a, b, dims=((1,), (0,))):
    return dot(a, b[0], dims) + dot(a, b[1], dims)


def fold_kernel(gradient, projector, own, s1, s2, s3):
    _, rows, _ = gradient.shape
    half = own.shape[1]
    me = lax.axis_index("tensor")
    for k, out in enumerate((own, s1, s2, s3)):
        peer = lax.rem(me + k, TENSOR)
        m, h = peer // 2, lax.rem(peer, 2)
        g = gradient[m]
        p = projector[m, :, pl.ds(pl.multiple_of(h * half, half), half)]
        f = dot_exact_left(g, split(p), ((0,), (0,)))
        if k == 0:
            out[...] = f
        else:
            out[:rows] = g.astype(F32)
            out[rows:] = f


def corrections(steps, m):
    one = jnp.float32(1.0)
    powers = lax.fori_loop(
        0, steps[m], lambda _, p: (p[0] * jnp.float32(BETA_ONE), p[1] * jnp.float32(BETA_TWO)), (one, one)
    )
    return 1.0 - powers[0], 1.0 - powers[1]


def pack_kernel(
    steps, first, second, gains, gain_gradient, gain_first, gain_second,
    pack, new_gains, new_gain_first, new_gain_second,
):
    mats, own_rank, _ = first.shape
    for i in range(mats):
        pack[i * own_rank : (i + 1) * own_rank] = first[i]
        pack[(mats + i) * own_rank : (mats + i + 1) * own_rank] = second[i]
    for i in range(mats):
        c1, c2 = corrections(steps, i)
        row = slice(i, i + 1)
        g = gain_gradient[row]
        n1 = BETA_ONE * gain_first[row] + (1.0 - BETA_ONE) * g
        n2 = BETA_TWO * gain_second[row] + (1.0 - BETA_TWO) * g * g
        new_gain_first[row] = n1
        new_gain_second[row] = n2
        new_gains[row] = gains[row] - LEARN_RATE * (n1 / c1) / (jnp.sqrt(n2 / c2) + EPSILON)


def range_kernel(gradient, own, r1, r2, r3, ranged):
    _, rows, _ = gradient.shape
    me = lax.axis_index("tensor")
    total = (own[...] + r1[rows:]) + (r2[rows:] + r3[rows:])
    total = split(total)
    for k, r in enumerate((None, r1, r2, r3)):
        peer = lax.rem(me + (TENSOR - k), TENSOR)
        g = gradient[me // 2] if k == 0 else r[:rows].astype(BF16)
        ranged[pl.ds(pl.multiple_of(peer * rows, 8), rows), :] = dot_exact_left(g, total)


def spread_kernel(parts, out):
    total = jnp.sum(parts[...], axis=0)
    for i in range(out.shape[0]):
        out[i] = total


def own_rows(gradient, r1, r2, r3):
    rows = gradient.shape[1]
    me = lax.axis_index("tensor")
    for k, r in enumerate((None, r1, r2, r3)):
        start = pl.multiple_of(lax.rem(me + (TENSOR - k), TENSOR) * rows, 8)
        yield start, gradient[me // 2] if k == 0 else r[:rows].astype(BF16)


def own_products_kernel(mine, gradient, r1, r2, r3, to_across, to_opposite):
    rows = gradient.shape[1]
    half = mine.shape[1]
    me = lax.axis_index("tensor")
    gram = jnp.zeros((half, half), F32)
    cross = jnp.zeros((half, gradient.shape[2]), F32)
    for start, g in own_rows(gradient, r1, r2, r3):
        ys = split(mine[pl.ds(start, rows), :])
        yt = (ys[0].T, ys[1].T)
        gram += dot3(yt, ys)
        cross += dot(yt[0], g) + dot(yt[1], g)
    for mask, out in ((3, to_across), (2, to_opposite)):
        peer = me ^ mask
        out[:half] = cross
        out[half : 2 * half] = gram
        out[2 * half :] = mine[pl.ds(pl.multiple_of(peer * rows, 8), rows), :]


def joint_products_kernel(mine, beside, gradient, r1, r2, r3, joint, near):
    rows = gradient.shape[1]
    half = mine.shape[1]
    between = jnp.zeros((half, half), F32)
    gram = jnp.zeros((half, half), F32)
    cross = jnp.zeros((half, gradient.shape[2]), F32)
    for start, g in own_rows(gradient, r1, r2, r3):
        at = pl.ds(start, rows)
        xs, ys = split(mine[at, :]), split(beside[at, :])
        xt, yt = (xs[0].T, xs[1].T), (ys[0].T, ys[1].T)
        between += dot3(xt, ys)
        gram += dot3(yt, ys)
        cross += dot(yt[0], g) + dot(yt[1], g)
    joint[...] = between
    near[:half] = cross
    near[half : 2 * half] = gram
    me = lax.axis_index("tensor")
    near[2 * half :] = beside[pl.ds(pl.multiple_of(me * rows, 8), rows), :]


def finish_kernel(
    other, same, swap, joint, first, second, weight, q1, q2, q3, steps, *rest,
):
    rest = list(rest)
    basis = None if other else rest.pop(0)
    earlier, outs = rest[:-8], rest[-8:-4]
    grams, crosses, direction_at, locals_ = rest[-4:]
    weight_next, fresh, new_first, new_second = outs
    mats, own_rank, _ = first.shape
    rows = weight.shape[1]
    half = joint.shape[1]
    rank = 2 * half
    me = lax.axis_index("tensor")
    mine = me // 2
    m = 1 - mine if other else mine
    h = lax.rem(me, 2)
    if earlier:
        for before, out in zip(earlier, outs):
            out[mine] = before[...]
        put = lambda ref, value: ref.__setitem__(m, value)
    else:
        put = lambda ref, value: ref.__setitem__(Ellipsis, value)
    here = pl.ds(pl.multiple_of(h * half, half), half)
    there = pl.ds(pl.multiple_of((1 - h) * half, half), half)
    grams[here, here] = same[half : 2 * half]
    grams[there, there] = swap[half : 2 * half]
    between = joint[...]
    if other:
        grams[there, here] = between
        grams[here, there] = between.T
        locals_[:, here] = same[2 * half :]
    else:
        grams[here, there] = between
        grams[there, here] = between.T
        locals_[:, here] = basis[pl.ds(pl.multiple_of(me * rows, 8), rows), :]
    locals_[:, there] = swap[2 * half :]
    crosses[here, :] = same[:half]
    crosses[there, :] = swap[:half]
    eye = (
        lax.broadcasted_iota(jnp.int32, (rank, rank), 0)
        == lax.broadcasted_iota(jnp.int32, (rank, rank), 1)
    ).astype(F32)
    gram = grams[...]
    inverse = 1.0 / (jnp.sqrt(jnp.sum(gram * eye)) + NORM_EPS)
    gram, cross, local = gram * (inverse * inverse), crosses[...] * inverse, locals_[...] * inverse
    for sweep in range(NS_STEPS):
        step = split(1.5 * eye - 0.5 * gram)
        cross = dot3(step, split(cross))
        local = dot3(split(local), step)
        if sweep < NS_STEPS - 1:
            gram = dot3(split(dot3(step, split(gram))), step)
    put(fresh, local)
    crosses[...] = cross
    c1, c2 = corrections(steps, m)
    for k, q in enumerate((None, q1, q2, q3)):
        peer = lax.rem(me + (TENSOR - k), TENSOR)
        at = pl.ds(pl.multiple_of(peer * own_rank, 8), own_rank)
        projected = crosses[at, :]
        if k == 0:
            m1, m2 = first[m], second[m]
        else:
            m1 = q[pl.ds(pl.multiple_of(m * own_rank, 8), own_rank), :]
            m2 = q[pl.ds(pl.multiple_of((mats + m) * own_rank, 8), own_rank), :]
        n1 = BETA_ONE * m1 + (1.0 - BETA_ONE) * projected
        n2 = BETA_TWO * m2 + (1.0 - BETA_TWO) * projected * projected
        if k == 0:
            put(new_first, n1)
            put(new_second, n2)
        direction_at[at, :] = n1 / c1 / (jnp.sqrt(n2 / c2) + EPSILON)
    update = dot3(split(local), split(direction_at[...]))
    w = weight[m].astype(F32)
    put(weight_next, (w - LEARN_RATE * (GALORE_SCALE * update + WEIGHT_DECAY * w)).astype(BF16))


def shards(
    gradient,
    weight,
    projector,
    first_moment,
    squared_moment,
    step_count,
    norm_gains,
    gain_gradient,
    gain_first,
    gain_second,
):
    mats, rows, cols = gradient.shape
    rank = projector.shape[2]
    own_rank = first_moment.shape[1]
    half = rank // 2
    spread = lax.axis_size("shards")
    block = TENSOR * rows // spread
    shape = jax.ShapeDtypeStruct

    def shifted(x, k):
        return lax.ppermute(x, "tensor", [(i, (i + k) % TENSOR) for i in range(TENSOR)])

    def swapped(x, mask):
        return lax.ppermute(x, "tensor", [(i, i ^ mask) for i in range(TENSOR)])

    def call(kernel, out_shape, inputs, mib, in_specs=None, **more):
        outs = out_shape if isinstance(out_shape, tuple) else (out_shape,)
        got = pl.pallas_call(
            kernel,
            out_shape=outs,
            in_specs=in_specs or [VMEM] * len(inputs),
            out_specs=(VMEM,) * len(outs),
            compiler_params=pltpu.CompilerParams(vmem_limit_bytes=mib << 20),
            **more,
        )(*inputs)
        return got if isinstance(out_shape, tuple) else got[0]

    own, s1, s2, s3 = call(
        fold_kernel,
        (shape((cols, half), F32),) + (shape((rows + cols, half), F32),) * 3,
        (gradient, projector),
        8,
    )
    r2, r3, r1 = shifted(s2, 2), shifted(s3, 3), shifted(s1, 1)
    small = shape(norm_gains.shape, F32)
    pack, new_gains, new_gain_first, new_gain_second = call(
        pack_kernel,
        (shape((2 * mats * own_rank, cols), F32),) + (small,) * 3,
        (
            step_count, first_moment, squared_moment,
            norm_gains, gain_gradient, gain_first, gain_second,
        ),
        8,
        in_specs=[SMEM] + [VMEM] * 6,
    )
    q2, q3, q1 = shifted(pack, 2), shifted(pack, 3), shifted(pack, 1)

    ranged_part = call(
        range_kernel, shape((TENSOR * rows, half), F32), (gradient, own, r1, r2, r3), 8
    )
    parts = lax.all_to_all(ranged_part, "shards", 0, 0, tiled=True)
    blocks = call(
        spread_kernel, shape((spread, block, half), F32), (parts.reshape(spread, block, half),), 8
    )
    mine = lax.all_to_all(
        blocks.reshape(spread * block, half), "shards", 0, 0, tiled=True
    )
    gradients = (gradient, r1, r2, r3)
    message = shape((2 * half + rows, half), F32)
    beside = swapped(mine, 1)
    to_across, to_opposite = call(own_products_kernel, (message,) * 2, (mine,) + gradients, 8)
    across, opposite = swapped(to_across, 3), swapped(to_opposite, 2)
    joint, near = call(
        joint_products_kernel, (shape((half, half), F32), message), (mine, beside) + gradients, 8
    )
    joint_across = swapped(joint, 3)
    shapes = [weight, projector, first_moment, squared_moment]
    scratch = [
        pltpu.VMEM((rank, rank), F32),
        pltpu.VMEM((rank, cols), F32),
        pltpu.VMEM((rank, cols), F32),
        pltpu.VMEM((rows, rank), F32),
    ]
    shared = (first_moment, squared_moment, weight, q1, q2, q3, step_count)
    specs = [VMEM] * 9 + [SMEM]
    done = call(
        functools.partial(finish_kernel, False),
        tuple(shape(x.shape[1:], x.dtype) for x in shapes),
        (to_across, near, joint) + shared + (mine,),
        16,
        in_specs=specs + [VMEM],
        scratch_shapes=scratch,
    )
    weight_next, fresh_projector, new_first, new_second = call(
        functools.partial(finish_kernel, True),
        tuple(shape(x.shape, x.dtype) for x in shapes),
        (opposite, across, joint_across) + shared + done,
        16,
        in_specs=specs + [VMEM] * 4,
        scratch_shapes=scratch,
    )
    return (
        weight_next,
        fresh_projector,
        new_first,
        new_second,
        new_gains,
        new_gain_first,
        new_gain_second,
    )


def solution(mesh):
    return jax.shard_map(
        shards,
        mesh=mesh,
        in_specs=(
            P("section", "tensor", "shards"),
            P("section", "tensor", "shards"),
            P("section", "tensor", None),
            P("section", "tensor", "shards"),
            P("section", "tensor", "shards"),
            P("section"),
            P("section", "tensor"),
            P("section", "tensor"),
            P("section", "tensor"),
            P("section", "tensor"),
        ),
        out_specs=(
            P("section", "tensor", "shards"),
            P("section", "tensor", None),
            P("section", "tensor", "shards"),
            P("section", "tensor", "shards"),
            P("section", "tensor"),
            P("section", "tensor"),
            P("section", "tensor"),
        ),
        check_vma=False,
    )
```

time: 79.2 us -> 75.5 us (0.953)
  waiting for transfers between devices: 24.7 us -> 11.7 us
  blocking collectives: 16 us -> 28.7 us
  other arithmetic: 2.69 us -> 0 us
  local copies, waits for them, and re-layouts: 4.51 us -> 1.92 us
  Pallas kernels: 10.5 us -> 12.5 us
    ppermute x6, waiting for transfers between devices: 24.7 us -> 9.98 us  [shifted(): lax.ppermute(x, 'tensor', [(i, (i + k) % TENSOR) for i in range(TENSOR)])]
    all_to_all x0 -> x1, blocking collectives: none -> 12.8 us  [shards(): lax.all_to_all(blocks.reshape(spread * block, half), 'shards', 0, 0, tile...]
    all_to_all x1 -> x0, starting transfers between devices: 6.91 us -> none  [shards(): lax.all_to_all(blocks.reshape(spread * TENSOR * block, half), ('tensor',...]
    ppermute x0 -> x4, starting transfers between devices: none -> 6.22 us  [swapped(): return lax.ppermute(x, 'tensor', [(i, i ^ mask) for i in range(TENSOR)])]
    sub x2 -> x0, local copies, waits for them, and re-layouts: 2.59 us -> none  [the longest x1 1.3 us: shards(): correct_one = 1.0 - BETA_ONE ** steps]
    pallas_call x5 -> x8, Pallas kernels: 10.5 us -> 12.5 us  [call(): pl.pallas_call(kernel, out_shape=outs, in_specs=in_specs or [VMEM] * len(...]
    sub x2 -> x0, other arithmetic: 1.92 us -> none  [the longest x1 1.39 us: shards(): norm_gains - LEARN_RATE * (new_gain_first / correct_one) / (jnp.sqrt(new_...]
    ppermute x0 -> x4, waiting for transfers between devices: none -> 1.74 us  [swapped(): return lax.ppermute(x, 'tensor', [(i, i ^ mask) for i in range(TENSOR)])]
  transfers between devices with their start and end apart: 7 -> 10, of which waited for: 4 -> 5; matrix products, arithmetic and copies ran while one was open for 7% -> 0% of each run, Pallas kernels for 1% -> 9%
where the time goes in v1:
time: 75.5 us; the launch traced here: 75.2 us
  blocking collectives  28.7 us (38%)
  starting transfers between devices  19.6 us (26%)
  Pallas kernels  12.5 us (17%)
  waiting for transfers between devices  11.7 us (15%)
  local copies, waits for them, and re-layouts  1.92 us (3%)
  between operations  0.77 us (1%)
    all_to_all x1, blocking collectives, shards(): parts = lax.all_to_all(ranged_part, 'shards', 0, 0, tiled=True)  16 us
    ppermute x6, starting transfers between devices, shifted(): lax.ppermute(x, 'tensor', [(i, (i + k) % TENSOR) for i in range(TENSOR)])  13.4 us
    all_to_all x1, blocking collectives, shards(): lax.all_to_all(blocks.reshape(spread * block, half), 'shards', 0, 0, tile...  12.8 us
    pallas_call x8, Pallas kernels, call(): pl.pallas_call(kernel, out_shape=outs, in_specs=in_specs or [VMEM] * len(...  12.5 us
    ppermute x6, waiting for transfers between devices, shifted(): lax.ppermute(x, 'tensor', [(i, (i + k) % TENSOR) for i in range(TENSOR)])  9.98 us
    ppermute x4, starting transfers between devices, swapped(): return lax.ppermute(x, 'tensor', [(i, i ^ mask) for i in range(TENSOR)])  6.22 us
    unnamed x22, local copies, waits for them, and re-layouts  1.92 us
    ppermute x4, waiting for transfers between devices, swapped(): return lax.ppermute(x, 'tensor', [(i, i ^ mask) for i in range(TENSOR)])  1.74 us
  transfers between devices with their start and end apart: 10, of which 5 were waited for; matrix products, arithmetic and copies ran while one was open for 0% of the time, Pallas kernels for 9%

profile of v1, /device:TPU:0, one launch (start us, length us, event | category | flops | bytes accessed | tf_op | source)
XLA Modules:
  0.0 75.2 jit_solution(2238372496370747634)
XLA Ops:
  0.6 0.0 copy-start
  0.6 0.9 %copy-done = bf16[2,192,128]{2,1,0:T(8,128)(2,1)S(1)} copy-done((bf16[2,192,128]{2,1,0:T(8,128)(2,1)S(1)}, bf16[2,192,128]{2,1,0:T(8,128)(2,1)}, u32[]{:S(2)}) %copy-start) | copy-done | bytes 98328
  1.5 0.0 copy-start.4
  1.5 1.0 %copy-done.4 = f32[2,192,256]{2,1,0:T(8,128)S(1)} copy-done((f32[2,192,256]{2,1,0:T(8,128)S(1)}, f32[2,192,256]{2,1,0:T(8,128)}, u32[]{:S(2)}) %copy-start.4) | copy-done | bytes 393240
  2.5 0.4 shard_map.153
  2.9 2.1 %collective-permute-start = (f32[320,128]{1,0:T(8,128)S(1)}, f32[320,128]{1,0:T(8,128)S(1)}, u32[]{:S(2)}, u32[]{:S(2)}) collective-permute-start(f32[320,128]{1,0:T(8,128)S(1)} %get-tuple-element.28), channel_id=1, source_target_pairs={{0,2},{2,4},{4,6},{6,0},{1,3},{3,5},{5,7},{7,1},{8,10},{10,12},{12... | collective-permute-start | bytes 491528 | tf_op jit(solution)/shard_map/ppermute | solution.py:247
  5.0 3.6 %collective-permute-start.1 = (f32[320,128]{1,0:T(8,128)S(1)}, f32[320,128]{1,0:T(8,128)S(1)}, u32[]{:S(2)}, u32[]{:S(2)}) collective-permute-start(f32[320,128]{1,0:T(8,128)S(1)} %get-tuple-element.29), channel_id=1, source_target_pairs={{0,4},{2,6},{4,0},{6,2},{1,5},{3,7},{5,1},{7,3},{8,12},{10,14},{12... | collective-permute-start | bytes 491528 | tf_op jit(solution)/shard_map/ppermute | solution.py:247
  8.6 1.0 %collective-permute-start.2 = (f32[320,128]{1,0:T(8,128)S(1)}, f32[320,128]{1,0:T(8,128)S(1)}, u32[]{:S(2)}, u32[]{:S(2)}) collective-permute-start(f32[320,128]{1,0:T(8,128)S(1)} %get-tuple-element.30), channel_id=1, source_target_pairs={{0,6},{2,0},{4,2},{6,4},{1,7},{3,1},{5,3},{7,5},{8,14},{10,8},{12,... | collective-permute-start | bytes 491528 | tf_op jit(solution)/shard_map/ppermute | solution.py:247
  9.6 1.7 %collective-permute-done.r1 = f32[320,128]{1,0:T(8,128)S(1)} collective-permute-done((f32[320,128]{1,0:T(8,128)S(1)}, f32[320,128]{1,0:T(8,128)S(1)}, u32[]{:S(2)}, u32[]{:S(2)}) %collective-permute-start) | collective-permute-done | bytes 163872 | tf_op jit(solution)/shard_map/ppermute | solution.py:247
  11.3 4.7 %collective-permute-done.1.r2 = f32[320,128]{1,0:T(8,128)S(1)} collective-permute-done((f32[320,128]{1,0:T(8,128)S(1)}, f32[320,128]{1,0:T(8,128)S(1)}, u32[]{:S(2)}, u32[]{:S(2)}) %collective-permute-start.1) | collective-permute-done | bytes 163872 | tf_op jit(solution)/shard_map/ppermute | solution.py:247
  16.0 0.0 collective-permute-done.2.r3
  16.0 0.3 shard_map.154
  16.3 16.0 %all_to_all.17.parts = f32[16,48,128]{2,1,0:T(8,128)S(1)} all-to-all(f32[16,48,128]{2,1,0:T(8,128)S(1)} %bitcast.6), channel_id=1, replica_groups=mesh['shards'=16,'tensor'=4,'section'=2] {'shards'}, dimensions={0} | all-to-all | bytes 786432 | tf_op jit(solution)/shard_map/all_to_all | solution.py:287
  32.3 0.0 copy-start.1
  32.3 12.8 %all_to_all.18 = f32[16,48,128]{2,1,0:T(8,128)S(1)} all-to-all(f32[16,48,128]{2,1,0:T(8,128)S(1)} %shard_map.155), channel_id=1, replica_groups=mesh['shards'=16,'tensor'=4,'section'=2] {'shards'}, dimensions={0} | all-to-all | bytes 786432 | tf_op jit(solution)/shard_map/all_to_all | solution.py:291
  45.1 0.0 copy-start.2
  45.1 0.0 copy-start.3
  45.1 1.7 %collective-permute-start.5 = (f32[768,128]{1,0:T(8,128)S(1)}, f32[768,128]{1,0:T(8,128)S(1)}, u32[]{:S(2)}, u32[]{:S(2)}) collective-permute-start(f32[768,128]{1,0:T(8,128)S(1)} %bitcast.2), channel_id=1, source_target_pairs={{0,2},{2,0},{4,6},{6,4},{1,3},{3,1},{5,7},{7,5},{8,10},{10,8},{12,... | collective-permute-start | bytes 1179656 | tf_op jit(solution)/shard_map/ppermute | solution.py:250
  46.8 0.0 copy-done.1
  46.8 0.0 copy-start.8
  46.8 0.6 shard_map.156
  47.4 0.0 copy-start.7
  47.4 0.0 copy-start.6
  47.4 1.1 %collective-permute-start.4 = (f32[448,128]{1,0:T(8,128)S(1)}, f32[448,128]{1,0:T(8,128)S(1)}, u32[]{:S(2)}, u32[]{:S(2)}) collective-permute-start(f32[448,128]{1,0:T(8,128)S(1)} %get-tuple-element.32.same), channel_id=1, source_target_pairs={{0,6},{2,4},{4,2},{6,0},{1,7},{3,5},{5,3},{7,1},{8,14},{10,12},{12... | collective-permute-start | bytes 688136 | tf_op jit(solution)/shard_map/ppermute | solution.py:250
  48.5 1.5 %collective-permute-start.3 = (f32[448,128]{1,0:T(8,128)S(1)}, f32[448,128]{1,0:T(8,128)S(1)}, u32[]{:S(2)}, u32[]{:S(2)}) collective-permute-start(f32[448,128]{1,0:T(8,128)S(1)} %get-tuple-element.31), channel_id=1, source_target_pairs={{0,4},{2,6},{4,0},{6,2},{1,5},{3,7},{5,1},{7,3},{8,12},{10,14},{12... | collective-permute-start | bytes 688136 | tf_op jit(solution)/shard_map/ppermute | solution.py:250
  50.0 0.0 copy-done.2
  50.0 0.0 copy-done.3
  50.0 0.0 copy-done.8
  50.0 0.0 copy-done.9
  50.0 0.0 copy-done.10
  50.0 0.0 copy-done.7
  50.0 0.0 copy-done.6
  50.1 1.2 %shard_map.158 = (f32[256,128]{1,0:T(8,128)S(1)}, f32[2,192]{1,0:T(2,128)}, f32[2,192]{1,0:T(2,128)}, f32[2,192]{1,0:T(2,128)}) custom-call(s32[2]{0:T(128)S(1)} %copy-done.6, f32[2,64,128]{2,1,0:T(8,128)S(1)} %copy-done.2, f32[2,64,128]{2,1,0:T(8,128)S(1)} %copy-done.3, f32[2,192]{1,0:T(2,128)S(1)} %copy-done.7, f32[2,192]{1,0:T(2,128)S(1)} %copy-done.8, ...), custom_call_target="tpu_custom_call" | custom-call | tf_op jit(solution)/shard_map/pallas_call | solution.py:254
  51.3 1.6 %collective-permute-start.7 = (f32[256,128]{1,0:T(8,128)S(1)}, f32[256,128]{1,0:T(8,128)S(1)}, u32[]{:S(2)}, u32[]{:S(2)}) collective-permute-start(f32[256,128]{1,0:T(8,128)S(1)} %get-tuple-element.34), channel_id=1, source_target_pairs={{0,2},{2,4},{4,6},{6,0},{1,3},{3,5},{5,7},{7,1},{8,10},{10,12},{12... | collective-permute-start | bytes 393224 | tf_op jit(solution)/shard_map/ppermute | solution.py:247
  52.9 2.4 %collective-permute-start.8 = (f32[256,128]{1,0:T(8,128)S(1)}, f32[256,128]{1,0:T(8,128)S(1)}, u32[]{:S(2)}, u32[]{:S(2)}) collective-permute-start(f32[256,128]{1,0:T(8,128)S(1)} %get-tuple-element.34), channel_id=1, source_target_pairs={{0,4},{2,6},{4,0},{6,2},{1,5},{3,7},{5,1},{7,3},{8,12},{10,14},{12... | collective-permute-start | bytes 393224 | tf_op jit(solution)/shard_map/ppermute | solution.py:247
  55.3 1.7 %collective-permute-done.5.beside = f32[768,128]{1,0:T(8,128)S(1)} collective-permute-done((f32[768,128]{1,0:T(8,128)S(1)}, f32[768,128]{1,0:T(8,128)S(1)}, u32[]{:S(2)}, u32[]{:S(2)}) %collective-permute-start.5) | collective-permute-done | bytes 393248 | tf_op jit(solution)/shard_map/ppermute | solution.py:250
  57.0 2.7 %collective-permute-start.9 = (f32[256,128]{1,0:T(8,128)S(1)}, f32[256,128]{1,0:T(8,128)S(1)}, u32[]{:S(2)}, u32[]{:S(2)}) collective-permute-start(f32[256,128]{1,0:T(8,128)S(1)} %get-tuple-element.34), channel_id=1, source_target_pairs={{0,6},{2,0},{4,2},{6,4},{1,7},{3,1},{5,3},{7,5},{8,14},{10,8},{12,... | collective-permute-start | bytes 393224 | tf_op jit(solution)/shard_map/ppermute | solution.py:247
  59.8 0.8 shard_map.157
  60.5 2.7 %collective-permute-done.7.q1 = f32[256,128]{1,0:T(8,128)S(1)} collective-permute-done((f32[256,128]{1,0:T(8,128)S(1)}, f32[256,128]{1,0:T(8,128)S(1)}, u32[]{:S(2)}, u32[]{:S(2)}) %collective-permute-start.7) | collective-permute-done | bytes 131104 | tf_op jit(solution)/shard_map/ppermute | solution.py:247
  63.2 1.9 %collective-permute-start.6 = (f32[128,128]{1,0:T(8,128)S(1)}, f32[128,128]{1,0:T(8,128)S(1)}, u32[]{:S(2)}, u32[]{:S(2)}) collective-permute-start(f32[128,128]{1,0:T(8,128)S(1)} %get-tuple-element.33.joint), channel_id=1, source_target_pairs={{0,6},{2,4},{4,2},{6,0},{1,7},{3,5},{5,3},{7,1},{8,14},{10,12},{12... | collective-permute-start | bytes 196616 | tf_op jit(solution)/shard_map/ppermute | solution.py:250
  65.1 0.8 %collective-permute-done.8.q2 = f32[256,128]{1,0:T(8,128)S(1)} collective-permute-done((f32[256,128]{1,0:T(8,128)S(1)}, f32[256,128]{1,0:T(8,128)S(1)}, u32[]{:S(2)}, u32[]{:S(2)}) %collective-permute-start.8) | collective-permute-done | bytes 131104 | tf_op jit(solution)/shard_map/ppermute | solution.py:247
  66.0 0.0 collective-permute-done.9.q3
  66.0 0.0 copy-done.5
  66.0 4.3 %shard_map.159 = (bf16[192,128]{1,0:T(8,128)(2,1)S(1)}, f32[192,256]{1,0:T(8,128)S(1)}, f32[64,128]{1,0:T(8,128)S(1)}, f32[64,128]{1,0:T(8,128)S(1)}) custom-call(f32[448,128]{1,0:T(8,128)S(1)} %get-tuple-element.32.same, f32[448,128]{1,0:T(8,128)S(1)} %get-tuple-element.35.swap, f32[128,128]{1,0:T(8,128)S(1)} %get-tuple-element.33.joint, ...), custom_call_target="tpu_custom_call" | custom-call | tf_op jit(solution)/shard_map/pallas_call | solution.py:254
  70.3 0.0 collective-permute-done.4.swap
  70.3 0.0 collective-permute-done.3.same
  70.3 0.0 collective-permute-done.6.joint
  70.3 4.9 %shard_map.160 = (bf16[2,192,128]{2,1,0:T(8,128)(2,1)}, f32[2,192,256]{2,1,0:T(8,128)}, f32[2,64,128]{2,1,0:T(8,128)}, f32[2,64,128]{2,1,0:T(8,128)}) custom-call(f32[448,128]{1,0:T(8,128)S(1)} %collective-permute-done.3.same, f32[448,128]{1,0:T(8,128)S(1)} %collective-permute-done.4.swap, f32[128,128]{1,0:T(8,128)S(1)} %collective-permute-done.6.joint, ...), custom_call_target="tpu_custom_call" | custom-call | tf_op jit(solution)/shard_map/pallas_call | solution.py:254
  (4 shorter events, 0.0 us)
Async XLA Ops:
  0.6 0.9 %copy-start = (bf16[2,192,128]{2,1,0:T(8,128)(2,1)S(1)}, bf16[2,192,128]{2,1,0:T(8,128)(2,1)}, u32[]{:S(2)}) copy-start(bf16[2,192,128]{2,1,0:T(8,128)(2,1)} %gradient.7) | copy-start | bytes 294916
  1.5 1.0 %copy-start.4 = (f32[2,192,256]{2,1,0:T(8,128)S(1)}, f32[2,192,256]{2,1,0:T(8,128)}, u32[]{:S(2)}) copy-start(f32[2,192,256]{2,1,0:T(8,128)} %projector.1) | copy-start | bytes 1179652
  2.9 8.4 %collective-permute-start = (f32[320,128]{1,0:T(8,128)S(1)}, f32[320,128]{1,0:T(8,128)S(1)}, u32[]{:S(2)}, u32[]{:S(2)}) collective-permute-start(f32[320,128]{1,0:T(8,128)S(1)} %get-tuple-element.28), channel_id=1, source_target_pairs={{0,2},{2,4},{4,6},{6,0},{1,3},{3,5},{5,7},{7,1},{8,10},{10,12},{12... | collective-permute-start | bytes 491528 | tf_op jit(solution)/shard_map/ppermute | solution.py:247
  5.0 11.0 %collective-permute-start.1 = (f32[320,128]{1,0:T(8,128)S(1)}, f32[320,128]{1,0:T(8,128)S(1)}, u32[]{:S(2)}, u32[]{:S(2)}) collective-permute-start(f32[320,128]{1,0:T(8,128)S(1)} %get-tuple-element.29), channel_id=1, source_target_pairs={{0,4},{2,6},{4,0},{6,2},{1,5},{3,7},{5,1},{7,3},{8,12},{10,14},{12... | collective-permute-start | bytes 491528 | tf_op jit(solution)/shard_map/ppermute | solution.py:247
  8.6 7.4 %collective-permute-start.2 = (f32[320,128]{1,0:T(8,128)S(1)}, f32[320,128]{1,0:T(8,128)S(1)}, u32[]{:S(2)}, u32[]{:S(2)}) collective-permute-start(f32[320,128]{1,0:T(8,128)S(1)} %get-tuple-element.30), channel_id=1, source_target_pairs={{0,6},{2,0},{4,2},{6,4},{1,7},{3,1},{5,3},{7,5},{8,14},{10,8},{12,... | collective-permute-start | bytes 491528 | tf_op jit(solution)/shard_map/ppermute | solution.py:247
  32.3 14.5 %copy-start.1 = (bf16[2,192,128]{2,1,0:T(8,128)(2,1)S(1)}, bf16[2,192,128]{2,1,0:T(8,128)(2,1)}, u32[]{:S(2)}) copy-start(bf16[2,192,128]{2,1,0:T(8,128)(2,1)} %gradient.7) | copy-start | bytes 294916
  45.1 5.0 %copy-start.2 = (f32[2,64,128]{2,1,0:T(8,128)S(1)}, f32[2,64,128]{2,1,0:T(8,128)}, u32[]{:S(2)}) copy-start(f32[2,64,128]{2,1,0:T(8,128)} %first.5) | copy-start | bytes 196612
  45.1 5.0 %copy-start.3 = (f32[2,64,128]{2,1,0:T(8,128)S(1)}, f32[2,64,128]{2,1,0:T(8,128)}, u32[]{:S(2)}) copy-start(f32[2,64,128]{2,1,0:T(8,128)} %second.5) | copy-start | bytes 196612
  45.1 12.0 %collective-permute-start.5 = (f32[768,128]{1,0:T(8,128)S(1)}, f32[768,128]{1,0:T(8,128)S(1)}, u32[]{:S(2)}, u32[]{:S(2)}) collective-permute-start(f32[768,128]{1,0:T(8,128)S(1)} %bitcast.2), channel_id=1, source_target_pairs={{0,2},{2,0},{4,6},{6,4},{1,3},{3,1},{5,7},{7,5},{8,10},{10,8},{12,... | collective-permute-start | bytes 1179656 | tf_op jit(solution)/shard_map/ppermute | solution.py:250
  46.8 3.2 %copy-start.8 = (f32[2,192]{1,0:T(2,128)S(1)}, f32[2,192]{1,0:T(2,128)}, u32[]{:S(2)}) copy-start(f32[2,192]{1,0:T(2,128)} %gain_gradient.1) | copy-start | bytes 4612
  46.8 3.2 %copy-start.9 = (f32[2,192]{1,0:T(2,128)S(1)}, f32[2,192]{1,0:T(2,128)}, u32[]{:S(2)}) copy-start(f32[2,192]{1,0:T(2,128)} %gain_first.1) | copy-start | bytes 4612
  46.8 3.2 %copy-start.10 = (f32[2,192]{1,0:T(2,128)S(1)}, f32[2,192]{1,0:T(2,128)}, u32[]{:S(2)}) copy-start(f32[2,192]{1,0:T(2,128)} %gain_second.1) | copy-start | bytes 4612
  47.4 2.6 %copy-start.7 = (f32[2,192]{1,0:T(2,128)S(1)}, f32[2,192]{1,0:T(2,128)}, u32[]{:S(2)}) copy-start(f32[2,192]{1,0:T(2,128)} %gains.1) | copy-start | bytes 4612
  47.4 2.6 %copy-start.6 = (s32[2]{0:T(128)S(1)}, s32[2]{0:T(128)}, u32[]{:S(2)}) copy-start(s32[2]{0:T(128)} %steps.5) | copy-start | bytes 28
  47.4 22.9 %collective-permute-start.4 = (f32[448,128]{1,0:T(8,128)S(1)}, f32[448,128]{1,0:T(8,128)S(1)}, u32[]{:S(2)}, u32[]{:S(2)}) collective-permute-start(f32[448,128]{1,0:T(8,128)S(1)} %get-tuple-element.32.same), channel_id=1, source_target_pairs={{0,6},{2,4},{4,2},{6,0},{1,7},{3,5},{5,3},{7,1},{8,14},{10,12},{12... | collective-permute-start | bytes 688136 | tf_op jit(solution)/shard_map/ppermute | solution.py:250
  48.5 21.7 %collective-permute-start.3 = (f32[448,128]{1,0:T(8,128)S(1)}, f32[448,128]{1,0:T(8,128)S(1)}, u32[]{:S(2)}, u32[]{:S(2)}) collective-permute-start(f32[448,128]{1,0:T(8,128)S(1)} %get-tuple-element.31), channel_id=1, source_target_pairs={{0,4},{2,6},{4,0},{6,2},{1,5},{3,7},{5,1},{7,3},{8,12},{10,14},{12... | collective-permute-start | bytes 688136 | tf_op jit(solution)/shard_map/ppermute | solution.py:250
  51.3 14.6 %copy-start.5 = (bf16[2,192,128]{2,1,0:T(8,128)(2,1)S(1)}, bf16[2,192,128]{2,1,0:T(8,128)(2,1)}, u32[]{:S(2)}) copy-start(bf16[2,192,128]{2,1,0:T(8,128)(2,1)} %weight.3) | copy-start | bytes 294916
  51.3 11.9 %collective-permute-start.7 = (f32[256,128]{1,0:T(8,128)S(1)}, f32[256,128]{1,0:T(8,128)S(1)}, u32[]{:S(2)}, u32[]{:S(2)}) collective-permute-start(f32[256,128]{1,0:T(8,128)S(1)} %get-tuple-element.34), channel_id=1, source_target_pairs={{0,2},{2,4},{4,6},{6,0},{1,3},{3,5},{5,7},{7,1},{8,10},{10,12},{12... | collective-permute-start | bytes 393224 | tf_op jit(solution)/shard_map/ppermute | solution.py:247
  52.9 13.1 %collective-permute-start.8 = (f32[256,128]{1,0:T(8,128)S(1)}, f32[256,128]{1,0:T(8,128)S(1)}, u32[]{:S(2)}, u32[]{:S(2)}) collective-permute-start(f32[256,128]{1,0:T(8,128)S(1)} %get-tuple-element.34), channel_id=1, source_target_pairs={{0,4},{2,6},{4,0},{6,2},{1,5},{3,7},{5,1},{7,3},{8,12},{10,14},{12... | collective-permute-start | bytes 393224 | tf_op jit(solution)/shard_map/ppermute | solution.py:247
  57.0 8.9 %collective-permute-start.9 = (f32[256,128]{1,0:T(8,128)S(1)}, f32[256,128]{1,0:T(8,128)S(1)}, u32[]{:S(2)}, u32[]{:S(2)}) collective-permute-start(f32[256,128]{1,0:T(8,128)S(1)} %get-tuple-element.34), channel_id=1, source_target_pairs={{0,6},{2,0},{4,2},{6,4},{1,7},{3,1},{5,3},{7,5},{8,14},{10,8},{12,... | collective-permute-start | bytes 393224 | tf_op jit(solution)/shard_map/ppermute | solution.py:247
  63.2 7.1 %collective-permute-start.6 = (f32[128,128]{1,0:T(8,128)S(1)}, f32[128,128]{1,0:T(8,128)S(1)}, u32[]{:S(2)}, u32[]{:S(2)}) collective-permute-start(f32[128,128]{1,0:T(8,128)S(1)} %get-tuple-element.33.joint), channel_id=1, source_target_pairs={{0,6},{2,4},{4,2},{6,0},{1,7},{3,5},{5,3},{7,1},{8,14},{10,12},{12... | collective-permute-start | bytes 196616 | tf_op jit(solution)/shard_map/ppermute | solution.py:250

commit v2 on v1

--- a/solution.py
+++ b/solution.py
@@ -1,5 +1,3 @@
-import functools
-
 import jax
 import jax.numpy as jnp
 from jax import lax
@@ -150,77 +148,82 @@
 
 
 def finish_kernel(
-    other, same, swap, joint, first, second, weight, q1, q2, q3, steps, *rest,
+    same_mine, swap_mine, joint_mine, same_other, swap_other, joint_other, basis,
+    first, second, weight, q1, q2, q3, steps,
+    weight_next, fresh, new_first, new_second,
+    grams, crosses, directions, locals_,
 ):
-    rest = list(rest)
-    basis = None if other else rest.pop(0)
-    earlier, outs = rest[:-8], rest[-8:-4]
-    grams, crosses, direction_at, locals_ = rest[-4:]
-    weight_next, fresh, new_first, new_second = outs
     mats, own_rank, _ = first.shape
     rows = weight.shape[1]
-    half = joint.shape[1]
+    half = joint_mine.shape[1]
     rank = 2 * half
     me = lax.axis_index("tensor")
-    mine = me // 2
-    m = 1 - mine if other else mine
     h = lax.rem(me, 2)
-    if earlier:
-        for before, out in zip(earlier, outs):
-            out[mine] = before[...]
-        put = lambda ref, value: ref.__setitem__(m, value)
-    else:
-        put = lambda ref, value: ref.__setitem__(Ellipsis, value)
     here = pl.ds(pl.multiple_of(h * half, half), half)
     there = pl.ds(pl.multiple_of((1 - h) * half, half), half)
-    grams[here, here] = same[half : 2 * half]
-    grams[there, there] = swap[half : 2 * half]
-    between = joint[...]
-    if other:
-        grams[there, here] = between
-        grams[here, there] = between.T
-        locals_[:, here] = same[2 * half :]
-    else:
-        grams[here, there] = between
-        grams[there, here] = between.T
-        locals_[:, here] = basis[pl.ds(pl.multiple_of(me * rows, 8), rows), :]
-    locals_[:, there] = swap[2 * half :]
-    crosses[here, :] = same[:half]
-    crosses[there, :] = swap[:half]
     eye = (
         lax.broadcasted_iota(jnp.int32, (rank, rank), 0)
         == lax.broadcasted_iota(jnp.int32, (rank, rank), 1)
     ).astype(F32)
-    gram = grams[...]
-    inverse = 1.0 / (jnp.sqrt(jnp.sum(gram * eye)) + NORM_EPS)
-    gram, cross, local = gram * (inverse * inverse), crosses[...] * inverse, locals_[...] * inverse
+    which = (me // 2, 1 - me // 2)
+    state = []
+    for i, (same, swap, joint) in enumerate(
+        ((same_mine, swap_mine, joint_mine), (same_other, swap_other, joint_other))
+    ):
+        grams[i, here, here] = same[half : 2 * half]
+        grams[i, there, there] = swap[half : 2 * half]
+        between = joint[...]
+        if i == 0:
+            grams[i, here, there] = between
+            grams[i, there, here] = between.T
+            locals_[i, :, here] = basis[pl.ds(pl.multiple_of(me * rows, 8), rows), :]
+        else:
+            grams[i, there, here] = between
+            grams[i, here, there] = between.T
+            locals_[i, :, here] = same[2 * half :]
+        locals_[i, :, there] = swap[2 * half :]
+        crosses[i, here, :] = same[:half]
+        crosses[i, there, :] = swap[:half]
+        gram = grams[i]
+        inverse = 1.0 / (jnp.sqrt(jnp.sum(gram * eye)) + NORM_EPS)
+        state.append((gram * (inverse * inverse), crosses[i] * inverse, locals_[i] * inverse))
     for sweep in range(NS_STEPS):
-        step = split(1.5 * eye - 0.5 * gram)
-        cross = dot3(step, split(cross))
-        local = dot3(split(local), step)
+        steps_ = [split(1.5 * eye - 0.5 * gram) for gram, _, _ in state]
         if sweep < NS_STEPS - 1:
-            gram = dot3(split(dot3(step, split(gram))), step)
-    put(fresh, local)
-    crosses[...] = cross
-    c1, c2 = corrections(steps, m)
-    for k, q in enumerate((None, q1, q2, q3)):
-        peer = lax.rem(me + (TENSOR - k), TENSOR)
-        at = pl.ds(pl.multiple_of(peer * own_rank, 8), own_rank)
-        projected = crosses[at, :]
-        if k == 0:
-            m1, m2 = first[m], second[m]
+            halfway = [split(dot3(p, split(s[0]))) for p, s in zip(steps_, state)]
+            grams_ = [dot3(x, p) for x, p in zip(halfway, steps_)]
         else:
-            m1 = q[pl.ds(pl.multiple_of(m * own_rank, 8), own_rank), :]
-            m2 = q[pl.ds(pl.multiple_of((mats + m) * own_rank, 8), own_rank), :]
-        n1 = BETA_ONE * m1 + (1.0 - BETA_ONE) * projected
-        n2 = BETA_TWO * m2 + (1.0 - BETA_TWO) * projected * projected
-        if k == 0:
-            put(new_first, n1)
-            put(new_second, n2)
-        direction_at[at, :] = n1 / c1 / (jnp.sqrt(n2 / c2) + EPSILON)
-    update = dot3(split(local), split(direction_at[...]))
-    w = weight[m].astype(F32)
-    put(weight_next, (w - LEARN_RATE * (GALORE_SCALE * update + WEIGHT_DECAY * w)).astype(BF16))
+            grams_ = [None] * mats
+        state = [
+            (gram, dot3(p, split(s[1])), dot3(split(s[2]), p))
+            for gram, p, s in zip(grams_, steps_, state)
+        ]
+    for i, m in enumerate(which):
+        _, cross, local = state[i]
+        fresh[m] = local
+        crosses[i] = cross
+        c1, c2 = corrections(steps, m)
+        for k, q in enumerate((None, q1, q2, q3)):
+            peer = lax.rem(me + (TENSOR - k), TENSOR)
+            at = pl.ds(pl.multiple_of(peer * own_rank, 8), own_rank)
+            projected = crosses[i, at, :]
+            if k == 0:
+                m1, m2 = first[m], second[m]
+            else:
+                m1 = q[pl.ds(pl.multiple_of(m * own_rank, 8), own_rank), :]
+                m2 = q[pl.ds(pl.multiple_of((mats + m) * own_rank, 8), own_rank), :]
+            n1 = BETA_ONE * m1 + (1.0 - BETA_ONE) * projected
+            n2 = BETA_TWO * m2 + (1.0 - BETA_TWO) * projected * projected
+            if k == 0:
+                new_first[m] = n1
+                new_second[m] = n2
+            directions[i, at, :] = n1 / c1 / (jnp.sqrt(n2 / c2) + EPSILON)
+    for i, m in enumerate(which):
+        update = dot3(split(state[i][2]), split(directions[i]))
+        w = weight[m].astype(F32)
+        weight_next[m] = (
+            w - LEARN_RATE * (GALORE_SCALE * update + WEIGHT_DECAY * w)
+        ).astype(BF16)
 
 
 def shards(
@@ -301,29 +304,21 @@
     )
     joint_across = swapped(joint, 3)
     shapes = [weight, projector, first_moment, squared_moment]
-    scratch = [
-        pltpu.VMEM((rank, rank), F32),
-        pltpu.VMEM((rank, cols), F32),
-        pltpu.VMEM((rank, cols), F32),
-        pltpu.VMEM((rows, rank), F32),
-    ]
-    shared = (first_moment, squared_moment, weight, q1, q2, q3, step_count)
-    specs = [VMEM] * 9 + [SMEM]
-    done = call(
-        functools.partial(finish_kernel, False),
-        tuple(shape(x.shape[1:], x.dtype) for x in shapes),
-        (to_across, near, joint) + shared + (mine,),
-        16,
-        in_specs=specs + [VMEM],
-        scratch_shapes=scratch,
-    )
     weight_next, fresh_projector, new_first, new_second = call(
-        functools.partial(finish_kernel, True),
+        finish_kernel,
         tuple(shape(x.shape, x.dtype) for x in shapes),
-        (opposite, across, joint_across) + shared + done,
-        16,
-        in_specs=specs + [VMEM] * 4,
-        scratch_shapes=scratch,
+        (
+            to_across, near, joint, opposite, across, joint_across, mine,
+            first_moment, squared_moment, weight, q1, q2, q3, step_count,
+        ),
+        24,
+        in_specs=[VMEM] * 13 + [SMEM],
+        scratch_shapes=[
+            pltpu.VMEM((mats, rank, rank), F32),
+            pltpu.VMEM((mats, rank, cols), F32),
+            pltpu.VMEM((mats, rank, cols), F32),
+            pltpu.VMEM((mats, rows, rank), F32),
+        ],
     )
     return (
         weight_next,

time: 75.5 us -> 75.7 us (level)
  waiting for transfers between devices: 11.7 us -> 15 us
  Pallas kernels: 12.5 us -> 9.45 us
    ppermute x4, waiting for transfers between devices: 1.74 us -> 4.81 us  [swapped(): return lax.ppermute(x, 'tensor', [(i, i ^ mask) for i in range(TENSOR)])]
    pallas_call x8 -> x7, Pallas kernels: 12.5 us -> 9.45 us  [call(): pl.pallas_call(kernel, out_shape=outs, in_specs=in_specs or [VMEM] * len(...]
    ppermute x6, starting transfers between devices: 13.4 us -> 11.2 us  [shifted(): lax.ppermute(x, 'tensor', [(i, (i + k) % TENSOR) for i in range(TENSOR)])]
    ppermute x4, starting transfers between devices: 6.22 us -> 8.43 us  [swapped(): return lax.ppermute(x, 'tensor', [(i, i ^ mask) for i in range(TENSOR)])]
  transfers between devices with their start and end apart: 10 -> 10, of which waited for: 5 -> 5; matrix products, arithmetic and copies ran while one was open for 0% -> 0% of each run, Pallas kernels for 9% -> 3%
where the time goes in v2:
time: 75.7 us; the launch traced here: 75.5 us
  blocking collectives  28.7 us (38%)
  starting transfers between devices  19.6 us (26%)
  waiting for transfers between devices  15 us (20%)
  Pallas kernels  9.45 us (12%)
  local copies, waits for them, and re-layouts  1.92 us (3%)
    all_to_all x1, blocking collectives, shards(): parts = lax.all_to_all(ranged_part, 'shards', 0, 0, tiled=True)  16 us
    all_to_all x1, blocking collectives, shards(): lax.all_to_all(blocks.reshape(spread * block, half), 'shards', 0, 0, tile...  12.8 us
    ppermute x6, starting transfers between devices, shifted(): lax.ppermute(x, 'tensor', [(i, (i + k) % TENSOR) for i in range(TENSOR)])  11.2 us
    ppermute x6, waiting for transfers between devices, shifted(): lax.ppermute(x, 'tensor', [(i, (i + k) % TENSOR) for i in range(TENSOR)])  10.2 us
    pallas_call x7, Pallas kernels, call(): pl.pallas_call(kernel, out_shape=outs, in_specs=in_specs or [VMEM] * len(...  9.45 us
    ppermute x4, starting transfers between devices, swapped(): return lax.ppermute(x, 'tensor', [(i, i ^ mask) for i in range(TENSOR)])  8.43 us
    ppermute x4, waiting for transfers between devices, swapped(): return lax.ppermute(x, 'tensor', [(i, i ^ mask) for i in range(TENSOR)])  4.81 us
    unnamed x22, local copies, waits for them, and re-layouts  1.92 us
  transfers between devices with their start and end apart: 10, of which 5 were waited for; matrix products, arithmetic and copies ran while one was open for 0% of the time, Pallas kernels for 3%

profile of v2, /device:TPU:0, one launch (start us, length us, event | category | flops | bytes accessed | tf_op | source)
XLA Modules:
  0.0 75.5 jit_solution(13116532242812781144)
XLA Ops:
  0.6 0.0 copy-start
  0.6 0.9 %copy-done = bf16[2,192,128]{2,1,0:T(8,128)(2,1)S(1)} copy-done((bf16[2,192,128]{2,1,0:T(8,128)(2,1)S(1)}, bf16[2,192,128]{2,1,0:T(8,128)(2,1)}, u32[]{:S(2)}) %copy-start) | copy-done | bytes 98328
  1.5 0.0 copy-start.2
  1.5 1.0 %copy-done.2 = f32[2,192,256]{2,1,0:T(8,128)S(1)} copy-done((f32[2,192,256]{2,1,0:T(8,128)S(1)}, f32[2,192,256]{2,1,0:T(8,128)}, u32[]{:S(2)}) %copy-start.2) | copy-done | bytes 393240
  2.5 0.4 shard_map.153
  2.9 2.1 %collective-permute-start = (f32[320,128]{1,0:T(8,128)S(1)}, f32[320,128]{1,0:T(8,128)S(1)}, u32[]{:S(2)}, u32[]{:S(2)}) collective-permute-start(f32[320,128]{1,0:T(8,128)S(1)} %get-tuple-element.24), channel_id=1, source_target_pairs={{0,2},{2,4},{4,6},{6,0},{1,3},{3,5},{5,7},{7,1},{8,10},{10,12},{12... | collective-permute-start | bytes 491528 | tf_op jit(solution)/shard_map/ppermute | solution.py:250
  5.0 3.6 %collective-permute-start.1 = (f32[320,128]{1,0:T(8,128)S(1)}, f32[320,128]{1,0:T(8,128)S(1)}, u32[]{:S(2)}, u32[]{:S(2)}) collective-permute-start(f32[320,128]{1,0:T(8,128)S(1)} %get-tuple-element.25), channel_id=1, source_target_pairs={{0,4},{2,6},{4,0},{6,2},{1,5},{3,7},{5,1},{7,3},{8,12},{10,14},{12... | collective-permute-start | bytes 491528 | tf_op jit(solution)/shard_map/ppermute | solution.py:250
  8.6 1.0 %collective-permute-start.2 = (f32[320,128]{1,0:T(8,128)S(1)}, f32[320,128]{1,0:T(8,128)S(1)}, u32[]{:S(2)}, u32[]{:S(2)}) collective-permute-start(f32[320,128]{1,0:T(8,128)S(1)} %get-tuple-element.26), channel_id=1, source_target_pairs={{0,6},{2,0},{4,2},{6,4},{1,7},{3,1},{5,3},{7,5},{8,14},{10,8},{12,... | collective-permute-start | bytes 491528 | tf_op jit(solution)/shard_map/ppermute | solution.py:250
  9.6 1.7 %collective-permute-done.r1 = f32[320,128]{1,0:T(8,128)S(1)} collective-permute-done((f32[320,128]{1,0:T(8,128)S(1)}, f32[320,128]{1,0:T(8,128)S(1)}, u32[]{:S(2)}, u32[]{:S(2)}) %collective-permute-start) | collective-permute-done | bytes 163872 | tf_op jit(solution)/shard_map/ppermute | solution.py:250
  11.3 4.7 %collective-permute-done.1.r2 = f32[320,128]{1,0:T(8,128)S(1)} collective-permute-done((f32[320,128]{1,0:T(8,128)S(1)}, f32[320,128]{1,0:T(8,128)S(1)}, u32[]{:S(2)}, u32[]{:S(2)}) %collective-permute-start.1) | collective-permute-done | bytes 163872 | tf_op jit(solution)/shard_map/ppermute | solution.py:250
  16.0 0.0 collective-permute-done.2.r3
  16.0 0.3 shard_map.154
  16.3 16.0 %all_to_all.17.parts = f32[16,48,128]{2,1,0:T(8,128)S(1)} all-to-all(f32[16,48,128]{2,1,0:T(8,128)S(1)} %bitcast.6), channel_id=1, replica_groups=mesh['shards'=16,'tensor'=4,'section'=2] {'shards'}, dimensions={0} | all-to-all | bytes 786432 | tf_op jit(solution)/shard_map/all_to_all | solution.py:290
  32.3 0.0 copy-start.1
  32.3 12.8 %all_to_all.18 = f32[16,48,128]{2,1,0:T(8,128)S(1)} all-to-all(f32[16,48,128]{2,1,0:T(8,128)S(1)} %shard_map.155), channel_id=1, replica_groups=mesh['shards'=16,'tensor'=4,'section'=2] {'shards'}, dimensions={0} | all-to-all | bytes 786432 | tf_op jit(solution)/shard_map/all_to_all | solution.py:294
  45.1 0.0 copy-start.3
  45.1 0.0 copy-start.4
  45.1 1.7 %collective-permute-start.3 = (f32[768,128]{1,0:T(8,128)S(1)}, f32[768,128]{1,0:T(8,128)S(1)}, u32[]{:S(2)}, u32[]{:S(2)}) collective-permute-start(f32[768,128]{1,0:T(8,128)S(1)} %bitcast.2), channel_id=1, source_target_pairs={{0,2},{2,0},{4,6},{6,4},{1,3},{3,1},{5,7},{7,5},{8,10},{10,8},{12,... | collective-permute-start | bytes 1179656 | tf_op jit(solution)/shard_map/ppermute | solution.py:253
  46.8 0.0 copy-done.1
  46.8 0.0 copy-start.7
  46.8 0.0 copy-start.8
  46.8 0.6 shard_map.156
  47.4 0.0 copy-start.6
  47.4 0.0 copy-start.10
  47.4 2.5 %collective-permute-start.4 = (f32[448,128]{1,0:T(8,128)S(1)}, f32[448,128]{1,0:T(8,128)S(1)}, u32[]{:S(2)}, u32[]{:S(2)}) collective-permute-start(f32[448,128]{1,0:T(8,128)S(1)} %get-tuple-element.30), channel_id=1, source_target_pairs={{0,4},{2,6},{4,0},{6,2},{1,5},{3,7},{5,1},{7,3},{8,12},{10,14},{12... | collective-permute-start | bytes 688136 | tf_op jit(solution)/shard_map/ppermute | solution.py:253
  49.9 0.5 collective-permute-start.5
  50.4 0.0 copy-done.3
  50.5 0.0 copy-done.4
  50.5 0.0 copy-done.7
  50.5 0.0 copy-done.8
  50.5 0.0 copy-done.9
  50.5 0.0 copy-done.6
  50.5 0.0 copy-done.10
  50.5 1.2 %shard_map.158 = (f32[256,128]{1,0:T(8,128)S(1)}, f32[2,192]{1,0:T(2,128)}, f32[2,192]{1,0:T(2,128)}, f32[2,192]{1,0:T(2,128)}) custom-call(s32[2]{0:T(128)S(1)} %copy-done.10, f32[2,64,128]{2,1,0:T(8,128)S(1)} %copy-done.3, f32[2,64,128]{2,1,0:T(8,128)S(1)} %copy-done.4, f32[2,192]{1,0:T(2,128)S(1)} %copy-done.6, f32[2,192]{1,0:T(2,128)S(1)} %copy-done.7, ...), custom_call_target="tpu_custom_call" | custom-call | tf_op jit(solution)/shard_map/pallas_call | solution.py:257
  51.7 2.7 %collective-permute-start.9 = (f32[256,128]{1,0:T(8,128)S(1)}, f32[256,128]{1,0:T(8,128)S(1)}, u32[]{:S(2)}, u32[]{:S(2)}) collective-permute-start(f32[256,128]{1,0:T(8,128)S(1)} %get-tuple-element.31), channel_id=1, source_target_pairs={{0,6},{2,0},{4,2},{6,4},{1,7},{3,1},{5,3},{7,5},{8,14},{10,8},{12,... | collective-permute-start | bytes 393224 | tf_op jit(solution)/shard_map/ppermute | solution.py:250
  54.5 0.0 collective-permute-start.8
  54.5 2.6 %collective-permute-done.3.beside = f32[768,128]{1,0:T(8,128)S(1)} collective-permute-done((f32[768,128]{1,0:T(8,128)S(1)}, f32[768,128]{1,0:T(8,128)S(1)}, u32[]{:S(2)}, u32[]{:S(2)}) %collective-permute-start.3) | collective-permute-done | bytes 393248 | tf_op jit(solution)/shard_map/ppermute | solution.py:253
  57.0 1.7 %collective-permute-start.7 = (f32[256,128]{1,0:T(8,128)S(1)}, f32[256,128]{1,0:T(8,128)S(1)}, u32[]{:S(2)}, u32[]{:S(2)}) collective-permute-start(f32[256,128]{1,0:T(8,128)S(1)} %get-tuple-element.31), channel_id=1, source_target_pairs={{0,2},{2,4},{4,6},{6,0},{1,3},{3,5},{5,7},{7,1},{8,10},{10,12},{12... | collective-permute-start | bytes 393224 | tf_op jit(solution)/shard_map/ppermute | solution.py:250
  58.8 0.7 shard_map.157
  59.5 3.8 %collective-permute-done.9.q3 = f32[256,128]{1,0:T(8,128)S(1)} collective-permute-done((f32[256,128]{1,0:T(8,128)S(1)}, f32[256,128]{1,0:T(8,128)S(1)}, u32[]{:S(2)}, u32[]{:S(2)}) %collective-permute-start.9) | collective-permute-done | bytes 131104 | tf_op jit(solution)/shard_map/ppermute | solution.py:250
  63.3 3.7 %collective-permute-start.6 = (f32[128,128]{1,0:T(8,128)S(1)}, f32[128,128]{1,0:T(8,128)S(1)}, u32[]{:S(2)}, u32[]{:S(2)}) collective-permute-start(f32[128,128]{1,0:T(8,128)S(1)} %get-tuple-element.29.joint_mine), channel_id=1, source_target_pairs={{0,6},{2,4},{4,2},{6,0},{1,7},{3,5},{5,3},{7,1},{8,14},{10,12},{12... | collective-permute-start | bytes 196616 | tf_op jit(solution)/shard_map/ppermute | solution.py:253
  67.0 0.0 collective-permute-done.8.q2
  67.0 0.0 collective-permute-done.7.q1
  67.0 0.0 collective-permute-done.4.same_other
  67.0 0.0 collective-permute-done.5.swap_other
  67.0 2.2 %collective-permute-done.6.joint_other = f32[128,128]{1,0:T(8,128)S(1)} collective-permute-done((f32[128,128]{1,0:T(8,128)S(1)}, f32[128,128]{1,0:T(8,128)S(1)}, u32[]{:S(2)}, u32[]{:S(2)}) %collective-permute-start.6) | collective-permute-done | bytes 65568 | tf_op jit(solution)/shard_map/ppermute | solution.py:253
  69.2 0.0 copy-done.5
  69.2 6.2 %shard_map.159 = (bf16[2,192,128]{2,1,0:T(8,128)(2,1)}, f32[2,192,256]{2,1,0:T(8,128)}, f32[2,64,128]{2,1,0:T(8,128)}, f32[2,64,128]{2,1,0:T(8,128)}) custom-call(f32[448,128]{1,0:T(8,128)S(1)} %get-tuple-element.27.same_mine, f32[448,128]{1,0:T(8,128)S(1)} %get-tuple-element.28.swap_mine, f32[128,128]{1,0:T(8,128)S(1)} %get-tuple-element.29.joint_mine, ...), custom_call_target="tpu_custom_call" | custom-call | tf_op jit(solution)/shard_map/pallas_call | solution.py:257
  (3 shorter events, 0.0 us)
Async XLA Ops:
  0.6 0.9 %copy-start = (bf16[2,192,128]{2,1,0:T(8,128)(2,1)S(1)}, bf16[2,192,128]{2,1,0:T(8,128)(2,1)}, u32[]{:S(2)}) copy-start(bf16[2,192,128]{2,1,0:T(8,128)(2,1)} %gradient.7) | copy-start | bytes 294916
  1.5 1.0 %copy-start.2 = (f32[2,192,256]{2,1,0:T(8,128)S(1)}, f32[2,192,256]{2,1,0:T(8,128)}, u32[]{:S(2)}) copy-start(f32[2,192,256]{2,1,0:T(8,128)} %projector.1) | copy-start | bytes 1179652
  2.9 8.4 %collective-permute-start = (f32[320,128]{1,0:T(8,128)S(1)}, f32[320,128]{1,0:T(8,128)S(1)}, u32[]{:S(2)}, u32[]{:S(2)}) collective-permute-start(f32[320,128]{1,0:T(8,128)S(1)} %get-tuple-element.24), channel_id=1, source_target_pairs={{0,2},{2,4},{4,6},{6,0},{1,3},{3,5},{5,7},{7,1},{8,10},{10,12},{12... | collective-permute-start | bytes 491528 | tf_op jit(solution)/shard_map/ppermute | solution.py:250
  5.0 11.0 %collective-permute-start.1 = (f32[320,128]{1,0:T(8,128)S(1)}, f32[320,128]{1,0:T(8,128)S(1)}, u32[]{:S(2)}, u32[]{:S(2)}) collective-permute-start(f32[320,128]{1,0:T(8,128)S(1)} %get-tuple-element.25), channel_id=1, source_target_pairs={{0,4},{2,6},{4,0},{6,2},{1,5},{3,7},{5,1},{7,3},{8,12},{10,14},{12... | collective-permute-start | bytes 491528 | tf_op jit(solution)/shard_map/ppermute | solution.py:250
  8.6 7.4 %collective-permute-start.2 = (f32[320,128]{1,0:T(8,128)S(1)}, f32[320,128]{1,0:T(8,128)S(1)}, u32[]{:S(2)}, u32[]{:S(2)}) collective-permute-start(f32[320,128]{1,0:T(8,128)S(1)} %get-tuple-element.26), channel_id=1, source_target_pairs={{0,6},{2,0},{4,2},{6,4},{1,7},{3,1},{5,3},{7,5},{8,14},{10,8},{12,... | collective-permute-start | bytes 491528 | tf_op jit(solution)/shard_map/ppermute | solution.py:250
  32.3 14.5 %copy-start.1 = (bf16[2,192,128]{2,1,0:T(8,128)(2,1)S(1)}, bf16[2,192,128]{2,1,0:T(8,128)(2,1)}, u32[]{:S(2)}) copy-start(bf16[2,192,128]{2,1,0:T(8,128)(2,1)} %gradient.7) | copy-start | bytes 294916
  45.1 5.4 %copy-start.3 = (f32[2,64,128]{2,1,0:T(8,128)S(1)}, f32[2,64,128]{2,1,0:T(8,128)}, u32[]{:S(2)}) copy-start(f32[2,64,128]{2,1,0:T(8,128)} %first.3) | copy-start | bytes 196612
  45.1 5.4 %copy-start.4 = (f32[2,64,128]{2,1,0:T(8,128)S(1)}, f32[2,64,128]{2,1,0:T(8,128)}, u32[]{:S(2)}) copy-start(f32[2,64,128]{2,1,0:T(8,128)} %second.3) | copy-start | bytes 196612
  45.1 12.0 %collective-permute-start.3 = (f32[768,128]{1,0:T(8,128)S(1)}, f32[768,128]{1,0:T(8,128)S(1)}, u32[]{:S(2)}, u32[]{:S(2)}) collective-permute-start(f32[768,128]{1,0:T(8,128)S(1)} %bitcast.2), channel_id=1, source_target_pairs={{0,2},{2,0},{4,6},{6,4},{1,3},{3,1},{5,7},{7,5},{8,10},{10,8},{12,... | collective-permute-start | bytes 1179656 | tf_op jit(solution)/shard_map/ppermute | solution.py:253
  46.8 3.6 %copy-start.7 = (f32[2,192]{1,0:T(2,128)S(1)}, f32[2,192]{1,0:T(2,128)}, u32[]{:S(2)}) copy-start(f32[2,192]{1,0:T(2,128)} %gain_gradient.1) | copy-start | bytes 4612
  46.8 3.6 %copy-start.8 = (f32[2,192]{1,0:T(2,128)S(1)}, f32[2,192]{1,0:T(2,128)}, u32[]{:S(2)}) copy-start(f32[2,192]{1,0:T(2,128)} %gain_first.1) | copy-start | bytes 4612
  46.8 3.7 %copy-start.9 = (f32[2,192]{1,0:T(2,128)S(1)}, f32[2,192]{1,0:T(2,128)}, u32[]{:S(2)}) copy-start(f32[2,192]{1,0:T(2,128)} %gain_second.1) | copy-start | bytes 4612
  47.4 3.1 %copy-start.6 = (f32[2,192]{1,0:T(2,128)S(1)}, f32[2,192]{1,0:T(2,128)}, u32[]{:S(2)}) copy-start(f32[2,192]{1,0:T(2,128)} %gains.1) | copy-start | bytes 4612
  47.4 3.1 %copy-start.10 = (s32[2]{0:T(128)S(1)}, s32[2]{0:T(128)}, u32[]{:S(2)}) copy-start(s32[2]{0:T(128)} %steps.3) | copy-start | bytes 28
  47.4 19.6 %collective-permute-start.4 = (f32[448,128]{1,0:T(8,128)S(1)}, f32[448,128]{1,0:T(8,128)S(1)}, u32[]{:S(2)}, u32[]{:S(2)}) collective-permute-start(f32[448,128]{1,0:T(8,128)S(1)} %get-tuple-element.30), channel_id=1, source_target_pairs={{0,4},{2,6},{4,0},{6,2},{1,5},{3,7},{5,1},{7,3},{8,12},{10,14},{12... | collective-permute-start | bytes 688136 | tf_op jit(solution)/shard_map/ppermute | solution.py:253
  49.9 17.1 %collective-permute-start.5 = (f32[448,128]{1,0:T(8,128)S(1)}, f32[448,128]{1,0:T(8,128)S(1)}, u32[]{:S(2)}, u32[]{:S(2)}) collective-permute-start(f32[448,128]{1,0:T(8,128)S(1)} %get-tuple-element.27.same_mine), channel_id=1, source_target_pairs={{0,6},{2,4},{4,2},{6,0},{1,7},{3,5},{5,3},{7,1},{8,14},{10,12},{12... | collective-permute-start | bytes 688136 | tf_op jit(solution)/shard_map/ppermute | solution.py:253
  51.7 17.5 %copy-start.5 = (bf16[2,192,128]{2,1,0:T(8,128)(2,1)S(1)}, bf16[2,192,128]{2,1,0:T(8,128)(2,1)}, u32[]{:S(2)}) copy-start(bf16[2,192,128]{2,1,0:T(8,128)(2,1)} %weight.1) | copy-start | bytes 294916
  51.7 11.6 %collective-permute-start.9 = (f32[256,128]{1,0:T(8,128)S(1)}, f32[256,128]{1,0:T(8,128)S(1)}, u32[]{:S(2)}, u32[]{:S(2)}) collective-permute-start(f32[256,128]{1,0:T(8,128)S(1)} %get-tuple-element.31), channel_id=1, source_target_pairs={{0,6},{2,0},{4,2},{6,4},{1,7},{3,1},{5,3},{7,5},{8,14},{10,8},{12,... | collective-permute-start | bytes 393224 | tf_op jit(solution)/shard_map/ppermute | solution.py:250
  54.5 12.6 %collective-permute-start.8 = (f32[256,128]{1,0:T(8,128)S(1)}, f32[256,128]{1,0:T(8,128)S(1)}, u32[]{:S(2)}, u32[]{:S(2)}) collective-permute-start(f32[256,128]{1,0:T(8,128)S(1)} %get-tuple-element.31), channel_id=1, source_target_pairs={{0,4},{2,6},{4,0},{6,2},{1,5},{3,7},{5,1},{7,3},{8,12},{10,14},{12... | collective-permute-start | bytes 393224 | tf_op jit(solution)/shard_map/ppermute | solution.py:250
  57.0 10.0 %collective-permute-start.7 = (f32[256,128]{1,0:T(8,128)S(1)}, f32[256,128]{1,0:T(8,128)S(1)}, u32[]{:S(2)}, u32[]{:S(2)}) collective-permute-start(f32[256,128]{1,0:T(8,128)S(1)} %get-tuple-element.31), channel_id=1, source_target_pairs={{0,2},{2,4},{4,6},{6,0},{1,3},{3,5},{5,7},{7,1},{8,10},{10,12},{12... | collective-permute-start | bytes 393224 | tf_op jit(solution)/shard_map/ppermute | solution.py:250
  63.3 5.9 %collective-permute-start.6 = (f32[128,128]{1,0:T(8,128)S(1)}, f32[128,128]{1,0:T(8,128)S(1)}, u32[]{:S(2)}, u32[]{:S(2)}) collective-permute-start(f32[128,128]{1,0:T(8,128)S(1)} %get-tuple-element.29.joint_mine), channel_id=1, source_target_pairs={{0,6},{2,4},{4,2},{6,0},{1,7},{3,5},{5,3},{7,1},{8,14},{10,12},{12... | collective-permute-start | bytes 196616 | tf_op jit(solution)/shard_map/ppermute | solution.py:253

commit v3 on v2

--- a/solution.py
+++ b/solution.py
@@ -147,57 +147,62 @@
     near[2 * half :] = beside[pl.ds(pl.multiple_of(me * rows, 8), rows), :]
 
 
-def finish_kernel(
-    same_mine, swap_mine, joint_mine, same_other, swap_other, joint_other, basis,
-    first, second, weight, q1, q2, q3, steps,
-    weight_next, fresh, new_first, new_second,
-    grams, crosses, directions, locals_,
-):
-    mats, own_rank, _ = first.shape
-    rows = weight.shape[1]
-    half = joint_mine.shape[1]
+def orthogonalize(own, same, swap, joint, here_rows, grams, crosses, locals_):
+    half = joint.shape[1]
     rank = 2 * half
-    me = lax.axis_index("tensor")
-    h = lax.rem(me, 2)
+    h = lax.rem(lax.axis_index("tensor"), 2)
     here = pl.ds(pl.multiple_of(h * half, half), half)
     there = pl.ds(pl.multiple_of((1 - h) * half, half), half)
     eye = (
         lax.broadcasted_iota(jnp.int32, (rank, rank), 0)
         == lax.broadcasted_iota(jnp.int32, (rank, rank), 1)
     ).astype(F32)
+    grams[here, here] = same[half : 2 * half]
+    grams[there, there] = swap[half : 2 * half]
+    between = joint[...]
+    first, second = (here, there) if own else (there, here)
+    grams[first, second] = between
+    grams[second, first] = between.T
+    locals_[:, here] = here_rows
+    locals_[:, there] = swap[2 * half :]
+    crosses[here, :] = same[:half]
+    crosses[there, :] = swap[:half]
+    gram = grams[...]
+    inverse = 1.0 / (jnp.sqrt(jnp.sum(gram * eye)) + NORM_EPS)
+    gram, cross, local = gram * (inverse * inverse), crosses[...] * inverse, locals_[...] * inverse
+    for sweep in range(NS_STEPS):
+        step = split(1.5 * eye - 0.5 * gram)
+        cross = dot3(step, split(cross))
+        local = dot3(split(local), step)
+        if sweep < NS_STEPS - 1:
+            gram = dot3(split(dot3(step, split(gram))), step)
+    return cross, local
+
+
+def own_basis_kernel(same, swap, joint, basis, cross, local, grams, crosses, locals_):
+    rows = local.shape[0]
+    me = lax.axis_index("tensor")
+    here_rows = basis[pl.ds(pl.multiple_of(me * rows, 8), rows), :]
+    cross[...], local[...] = orthogonalize(
+        True, same, swap, joint, here_rows, grams, crosses, locals_
+    )
+
+
+def finish_kernel(
+    own_cross, own_local, same_other, swap_other, joint_other,
+    first, second, weight, q1, q2, q3, steps,
+    weight_next, fresh, new_first, new_second,
+    crosses, directions, grams, other_crosses, locals_,
+):
+    mats, own_rank, _ = first.shape
+    half = joint_other.shape[1]
+    me = lax.axis_index("tensor")
     which = (me // 2, 1 - me // 2)
-    state = []
-    for i, (same, swap, joint) in enumerate(
-        ((same_mine, swap_mine, joint_mine), (same_other, swap_other, joint_other))
-    ):
-        grams[i, here, here] = same[half : 2 * half]
-        grams[i, there, there] = swap[half : 2 * half]
-        between = joint[...]
-        if i == 0:
-            grams[i, here, there] = between
-            grams[i, there, here] = between.T
-            locals_[i, :, here] = basis[pl.ds(pl.multiple_of(me * rows, 8), rows), :]
-        else:
-            grams[i, there, here] = between
-            grams[i, here, there] = between.T
-            locals_[i, :, here] = same[2 * half :]
-        locals_[i, :, there] = swap[2 * half :]
-        crosses[i, here, :] = same[:half]
-        crosses[i, there, :] = swap[:half]
-        gram = grams[i]
-        inverse = 1.0 / (jnp.sqrt(jnp.sum(gram * eye)) + NORM_EPS)
-        state.append((gram * (inverse * inverse), crosses[i] * inverse, locals_[i] * inverse))
-    for sweep in range(NS_STEPS):
-        steps_ = [split(1.5 * eye - 0.5 * gram) for gram, _, _ in state]
-        if sweep < NS_STEPS - 1:
-            halfway = [split(dot3(p, split(s[0]))) for p, s in zip(steps_, state)]
-            grams_ = [dot3(x, p) for x, p in zip(halfway, steps_)]
-        else:
-            grams_ = [None] * mats
-        state = [
-            (gram, dot3(p, split(s[1])), dot3(split(s[2]), p))
-            for gram, p, s in zip(grams_, steps_, state)
-        ]
+    other = orthogonalize(
+        False, same_other, swap_other, joint_other, same_other[2 * half :],
+        grams, other_crosses, locals_,
+    )
+    state = [(None, own_cross[...], own_local[...]), (None,) + other]
     for i, m in enumerate(which):
         _, cross, local = state[i]
         fresh[m] = local
@@ -304,21 +309,28 @@
     )
     joint_across = swapped(joint, 3)
     shapes = [weight, projector, first_moment, squared_moment]
+    scratch = [
+        pltpu.VMEM((rank, rank), F32),
+        pltpu.VMEM((rank, cols), F32),
+        pltpu.VMEM((rows, rank), F32),
+    ]
+    own_state = call(
+        own_basis_kernel,
+        (shape((rank, cols), F32), shape((rows, rank), F32)),
+        (to_across, near, joint, mine),
+        16,
+        scratch_shapes=scratch,
+    )
     weight_next, fresh_projector, new_first, new_second = call(
         finish_kernel,
         tuple(shape(x.shape, x.dtype) for x in shapes),
-        (
-            to_across, near, joint, opposite, across, joint_across, mine,
+        tuple(own_state) + (
+            opposite, across, joint_across,
             first_moment, squared_moment, weight, q1, q2, q3, step_count,
         ),
         24,
-        in_specs=[VMEM] * 13 + [SMEM],
-        scratch_shapes=[
-            pltpu.VMEM((mats, rank, rank), F32),
-            pltpu.VMEM((mats, rank, cols), F32),
-            pltpu.VMEM((mats, rank, cols), F32),
-            pltpu.VMEM((mats, rows, rank), F32),
-        ],
+        in_specs=[VMEM] * 11 + [SMEM],
+        scratch_shapes=[pltpu.VMEM((mats, rank, cols), F32)] * 2 + scratch,
     )
     return (
         weight_next,

time: 75.7 us -> 74.1 us (0.979)
  waiting for transfers between devices: 15 us -> 11.1 us
  Pallas kernels: 9.45 us -> 11.7 us
    ppermute x4, waiting for transfers between devices: 4.81 us -> 1.99 us  [swapped(): return lax.ppermute(x, 'tensor', [(i, i ^ mask) for i in range(TENSOR)])]
    ppermute x6, starting transfers between devices: 11.2 us -> 13.4 us  [shifted(): lax.ppermute(x, 'tensor', [(i, (i + k) % TENSOR) for i in range(TENSOR)])]
    pallas_call x7 -> x8, Pallas kernels: 9.45 us -> 11.7 us  [call(): pl.pallas_call(kernel, out_shape=outs, in_specs=in_specs or [VMEM] * len(...]
    ppermute x4, starting transfers between devices: 8.43 us -> 6.22 us  [swapped(): return lax.ppermute(x, 'tensor', [(i, i ^ mask) for i in range(TENSOR)])]
    ppermute x6, waiting for transfers between devices: 10.2 us -> 9.14 us  [shifted(): lax.ppermute(x, 'tensor', [(i, (i + k) % TENSOR) for i in range(TENSOR)])]
  transfers between devices with their start and end apart: 10 -> 10, of which waited for: 5 -> 5; matrix products, arithmetic and copies ran while one was open for 0% -> 0% of each run, Pallas kernels for 3% -> 8%
where the time goes in v3:
time: 74.1 us; the launch traced here: 73.9 us
  blocking collectives  28.7 us (39%)
  starting transfers between devices  19.6 us (26%)
  Pallas kernels  11.7 us (16%)
  waiting for transfers between devices  11.1 us (15%)
  local copies, waits for them, and re-layouts  1.92 us (3%)
  between operations  0.78 us (1%)
    all_to_all x1, blocking collectives, shards(): parts = lax.all_to_all(ranged_part, 'shards', 0, 0, tiled=True)  16 us
    ppermute x6, starting transfers between devices, shifted(): lax.ppermute(x, 'tensor', [(i, (i + k) % TENSOR) for i in range(TENSOR)])  13.4 us
    all_to_all x1, blocking collectives, shards(): lax.all_to_all(blocks.reshape(spread * block, half), 'shards', 0, 0, tile...  12.8 us
    pallas_call x8, Pallas kernels, call(): pl.pallas_call(kernel, out_shape=outs, in_specs=in_specs or [VMEM] * len(...  11.7 us
    ppermute x6, waiting for transfers between devices, shifted(): lax.ppermute(x, 'tensor', [(i, (i + k) % TENSOR) for i in range(TENSOR)])  9.14 us
    ppermute x4, starting transfers between devices, swapped(): return lax.ppermute(x, 'tensor', [(i, i ^ mask) for i in range(TENSOR)])  6.22 us
    ppermute x4, waiting for transfers between devices, swapped(): return lax.ppermute(x, 'tensor', [(i, i ^ mask) for i in range(TENSOR)])  1.99 us
    unnamed x22, local copies, waits for them, and re-layouts  1.92 us
  transfers between devices with their start and end apart: 10, of which 5 were waited for; matrix products, arithmetic and copies ran while one was open for 0% of the time, Pallas kernels for 8%

profile of v3, /device:TPU:0, one launch (start us, length us, event | category | flops | bytes accessed | tf_op | source)
XLA Modules:
  0.0 73.9 jit_solution(9453619578633453714)
XLA Ops:
  0.6 0.0 copy-start
  0.6 0.9 %copy-done = bf16[2,192,128]{2,1,0:T(8,128)(2,1)S(1)} copy-done((bf16[2,192,128]{2,1,0:T(8,128)(2,1)S(1)}, bf16[2,192,128]{2,1,0:T(8,128)(2,1)}, u32[]{:S(2)}) %copy-start) | copy-done | bytes 98328
  1.5 0.0 copy-start.2
  1.5 1.0 %copy-done.2 = f32[2,192,256]{2,1,0:T(8,128)S(1)} copy-done((f32[2,192,256]{2,1,0:T(8,128)S(1)}, f32[2,192,256]{2,1,0:T(8,128)}, u32[]{:S(2)}) %copy-start.2) | copy-done | bytes 393240
  2.5 0.4 shard_map.153
  2.9 2.1 %collective-permute-start = (f32[320,128]{1,0:T(8,128)S(1)}, f32[320,128]{1,0:T(8,128)S(1)}, u32[]{:S(2)}, u32[]{:S(2)}) collective-permute-start(f32[320,128]{1,0:T(8,128)S(1)} %get-tuple-element.26), channel_id=1, source_target_pairs={{0,2},{2,4},{4,6},{6,0},{1,3},{3,5},{5,7},{7,1},{8,10},{10,12},{12... | collective-permute-start | bytes 491528 | tf_op jit(solution)/shard_map/ppermute | solution.py:255
  5.0 3.6 %collective-permute-start.1 = (f32[320,128]{1,0:T(8,128)S(1)}, f32[320,128]{1,0:T(8,128)S(1)}, u32[]{:S(2)}, u32[]{:S(2)}) collective-permute-start(f32[320,128]{1,0:T(8,128)S(1)} %get-tuple-element.27), channel_id=1, source_target_pairs={{0,4},{2,6},{4,0},{6,2},{1,5},{3,7},{5,1},{7,3},{8,12},{10,14},{12... | collective-permute-start | bytes 491528 | tf_op jit(solution)/shard_map/ppermute | solution.py:255
  8.6 1.0 %collective-permute-start.2 = (f32[320,128]{1,0:T(8,128)S(1)}, f32[320,128]{1,0:T(8,128)S(1)}, u32[]{:S(2)}, u32[]{:S(2)}) collective-permute-start(f32[320,128]{1,0:T(8,128)S(1)} %get-tuple-element.28), channel_id=1, source_target_pairs={{0,6},{2,0},{4,2},{6,4},{1,7},{3,1},{5,3},{7,5},{8,14},{10,8},{12,... | collective-permute-start | bytes 491528 | tf_op jit(solution)/shard_map/ppermute | solution.py:255
  9.6 1.7 %collective-permute-done.r1 = f32[320,128]{1,0:T(8,128)S(1)} collective-permute-done((f32[320,128]{1,0:T(8,128)S(1)}, f32[320,128]{1,0:T(8,128)S(1)}, u32[]{:S(2)}, u32[]{:S(2)}) %collective-permute-start) | collective-permute-done | bytes 163872 | tf_op jit(solution)/shard_map/ppermute | solution.py:255
  11.3 4.7 %collective-permute-done.1.r2 = f32[320,128]{1,0:T(8,128)S(1)} collective-permute-done((f32[320,128]{1,0:T(8,128)S(1)}, f32[320,128]{1,0:T(8,128)S(1)}, u32[]{:S(2)}, u32[]{:S(2)}) %collective-permute-start.1) | collective-permute-done | bytes 163872 | tf_op jit(solution)/shard_map/ppermute | solution.py:255
  16.0 0.0 collective-permute-done.2.r3
  16.0 0.3 shard_map.154
  16.3 16.0 %all_to_all.17.parts = f32[16,48,128]{2,1,0:T(8,128)S(1)} all-to-all(f32[16,48,128]{2,1,0:T(8,128)S(1)} %bitcast.6), channel_id=1, replica_groups=mesh['shards'=16,'tensor'=4,'section'=2] {'shards'}, dimensions={0} | all-to-all | bytes 786432 | tf_op jit(solution)/shard_map/all_to_all | solution.py:295
  32.3 0.0 copy-start.1
  32.3 12.8 %all_to_all.18 = f32[16,48,128]{2,1,0:T(8,128)S(1)} all-to-all(f32[16,48,128]{2,1,0:T(8,128)S(1)} %shard_map.155), channel_id=1, replica_groups=mesh['shards'=16,'tensor'=4,'section'=2] {'shards'}, dimensions={0} | all-to-all | bytes 786432 | tf_op jit(solution)/shard_map/all_to_all | solution.py:299
  45.1 0.0 copy-start.3
  45.1 0.0 copy-start.4
  45.1 1.7 %collective-permute-start.3 = (f32[768,128]{1,0:T(8,128)S(1)}, f32[768,128]{1,0:T(8,128)S(1)}, u32[]{:S(2)}, u32[]{:S(2)}) collective-permute-start(f32[768,128]{1,0:T(8,128)S(1)} %bitcast.2), channel_id=1, source_target_pairs={{0,2},{2,0},{4,6},{6,4},{1,3},{3,1},{5,7},{7,5},{8,10},{10,8},{12,... | collective-permute-start | bytes 1179656 | tf_op jit(solution)/shard_map/ppermute | solution.py:258
  46.8 0.0 copy-done.1
  46.8 0.0 copy-start.7
  46.8 0.6 shard_map.156
  47.4 0.0 copy-start.6
  47.4 0.0 copy-start.10
  47.4 1.1 %collective-permute-start.5 = (f32[448,128]{1,0:T(8,128)S(1)}, f32[448,128]{1,0:T(8,128)S(1)}, u32[]{:S(2)}, u32[]{:S(2)}) collective-permute-start(f32[448,128]{1,0:T(8,128)S(1)} %get-tuple-element.29.same), channel_id=1, source_target_pairs={{0,6},{2,4},{4,2},{6,0},{1,7},{3,5},{5,3},{7,1},{8,14},{10,12},{12... | collective-permute-start | bytes 688136 | tf_op jit(solution)/shard_map/ppermute | solution.py:258
  48.5 1.5 %collective-permute-start.4 = (f32[448,128]{1,0:T(8,128)S(1)}, f32[448,128]{1,0:T(8,128)S(1)}, u32[]{:S(2)}, u32[]{:S(2)}) collective-permute-start(f32[448,128]{1,0:T(8,128)S(1)} %get-tuple-element.34), channel_id=1, source_target_pairs={{0,4},{2,6},{4,0},{6,2},{1,5},{3,7},{5,1},{7,3},{8,12},{10,14},{12... | collective-permute-start | bytes 688136 | tf_op jit(solution)/shard_map/ppermute | solution.py:258
  50.0 0.0 copy-done.3
  50.0 0.0 copy-done.4
  50.0 0.0 copy-done.7
  50.0 0.0 copy-done.8
  50.0 0.0 copy-done.9
  50.0 0.0 copy-done.6
  50.0 0.0 copy-done.10
  50.1 1.2 %shard_map.159 = (f32[256,128]{1,0:T(8,128)S(1)}, f32[2,192]{1,0:T(2,128)}, f32[2,192]{1,0:T(2,128)}, f32[2,192]{1,0:T(2,128)}) custom-call(s32[2]{0:T(128)S(1)} %copy-done.10, f32[2,64,128]{2,1,0:T(8,128)S(1)} %copy-done.3, f32[2,64,128]{2,1,0:T(8,128)S(1)} %copy-done.4, f32[2,192]{1,0:T(2,128)S(1)} %copy-done.6, f32[2,192]{1,0:T(2,128)S(1)} %copy-done.7, ...), custom_call_target="tpu_custom_call" | custom-call | tf_op jit(solution)/shard_map/pallas_call | solution.py:262
  51.3 1.6 %collective-permute-start.7 = (f32[256,128]{1,0:T(8,128)S(1)}, f32[256,128]{1,0:T(8,128)S(1)}, u32[]{:S(2)}, u32[]{:S(2)}) collective-permute-start(f32[256,128]{1,0:T(8,128)S(1)} %get-tuple-element.35), channel_id=1, source_target_pairs={{0,2},{2,4},{4,6},{6,0},{1,3},{3,5},{5,7},{7,1},{8,10},{10,12},{12... | collective-permute-start | bytes 393224 | tf_op jit(solution)/shard_map/ppermute | solution.py:255
  52.9 2.4 %collective-permute-start.8 = (f32[256,128]{1,0:T(8,128)S(1)}, f32[256,128]{1,0:T(8,128)S(1)}, u32[]{:S(2)}, u32[]{:S(2)}) collective-permute-start(f32[256,128]{1,0:T(8,128)S(1)} %get-tuple-element.35), channel_id=1, source_target_pairs={{0,4},{2,6},{4,0},{6,2},{1,5},{3,7},{5,1},{7,3},{8,12},{10,14},{12... | collective-permute-start | bytes 393224 | tf_op jit(solution)/shard_map/ppermute | solution.py:255
  55.3 1.7 %collective-permute-done.3.beside = f32[768,128]{1,0:T(8,128)S(1)} collective-permute-done((f32[768,128]{1,0:T(8,128)S(1)}, f32[768,128]{1,0:T(8,128)S(1)}, u32[]{:S(2)}, u32[]{:S(2)}) %collective-permute-start.3) | collective-permute-done | bytes 393248 | tf_op jit(solution)/shard_map/ppermute | solution.py:258
  57.0 2.7 %collective-permute-start.9 = (f32[256,128]{1,0:T(8,128)S(1)}, f32[256,128]{1,0:T(8,128)S(1)}, u32[]{:S(2)}, u32[]{:S(2)}) collective-permute-start(f32[256,128]{1,0:T(8,128)S(1)} %get-tuple-element.35), channel_id=1, source_target_pairs={{0,6},{2,0},{4,2},{6,4},{1,7},{3,1},{5,3},{7,5},{8,14},{10,8},{12,... | collective-permute-start | bytes 393224 | tf_op jit(solution)/shard_map/ppermute | solution.py:255
  59.8 0.7 %shard_map.157 = (f32[128,128]{1,0:T(8,128)S(1)}, f32[448,128]{1,0:T(8,128)S(1)}) custom-call(f32[768,128]{1,0:T(8,128)S(1)} %bitcast.4, f32[768,128]{1,0:T(8,128)S(1)} %collective-permute-done.3.beside, bf16[2,192,128]{2,1,0:T(8,128)(2,1)S(1)} %copy-done.1, f32[320,128]{1,0:T(8,128)S(1)} %collective-permute-done.r1, ...), custom_call_target="tpu_custom_call" | custom-call | tf_op jit(solution)/shard_map/pallas_call | solution.py:262
  60.5 2.7 %collective-permute-done.7.q1 = f32[256,128]{1,0:T(8,128)S(1)} collective-permute-done((f32[256,128]{1,0:T(8,128)S(1)}, f32[256,128]{1,0:T(8,128)S(1)}, u32[]{:S(2)}, u32[]{:S(2)}) %collective-permute-start.7) | collective-permute-done | bytes 131104 | tf_op jit(solution)/shard_map/ppermute | solution.py:255
  63.2 1.9 %collective-permute-start.6 = (f32[128,128]{1,0:T(8,128)S(1)}, f32[128,128]{1,0:T(8,128)S(1)}, u32[]{:S(2)}, u32[]{:S(2)}) collective-permute-start(f32[128,128]{1,0:T(8,128)S(1)} %get-tuple-element.31.joint), channel_id=1, source_target_pairs={{0,6},{2,4},{4,2},{6,0},{1,7},{3,5},{5,3},{7,1},{8,14},{10,12},{12... | collective-permute-start | bytes 196616 | tf_op jit(solution)/shard_map/ppermute | solution.py:258
  65.1 3.3 %shard_map.158 = (f32[256,128]{1,0:T(8,128)S(1)}, f32[192,256]{1,0:T(8,128)S(1)}) custom-call(f32[448,128]{1,0:T(8,128)S(1)} %get-tuple-element.29.same, f32[448,128]{1,0:T(8,128)S(1)} %get-tuple-element.30.swap, f32[128,128]{1,0:T(8,128)S(1)} %get-tuple-element.31.joint, f32[768,128]{1,0:T(8,128)S(1)} %bitcast.5), custom_call_target="tpu_custom_call" | custom-call | tf_op jit(solution)/shard_map/pallas_call | solution.py:262
  68.4 0.0 collective-permute-done.8.q2
  68.4 0.0 collective-permute-done.9.q3
  68.4 0.0 collective-permute-done.5.swap_other
  68.5 0.0 collective-permute-done.4.same_other
  68.5 0.2 collective-permute-done.6.joint_other
  68.7 0.0 copy-done.5
  68.7 5.2 %shard_map.160 = (bf16[2,192,128]{2,1,0:T(8,128)(2,1)}, f32[2,192,256]{2,1,0:T(8,128)}, f32[2,64,128]{2,1,0:T(8,128)}, f32[2,64,128]{2,1,0:T(8,128)}) custom-call(f32[256,128]{1,0:T(8,128)S(1)} %get-tuple-element.32.own_cross, f32[192,256]{1,0:T(8,128)S(1)} %get-tuple-element.33.own_local, f32[448,128]{1,0:T(8,128)S(1)} %collective-permute-done.4.same_other, ...), custom_call_target="tpu_custom_call" | custom-call | tf_op jit(solution)/shard_map/pallas_call | solution.py:262
  (4 shorter events, 0.0 us)
Async XLA Ops:
  0.6 0.9 %copy-start = (bf16[2,192,128]{2,1,0:T(8,128)(2,1)S(1)}, bf16[2,192,128]{2,1,0:T(8,128)(2,1)}, u32[]{:S(2)}) copy-start(bf16[2,192,128]{2,1,0:T(8,128)(2,1)} %gradient.7) | copy-start | bytes 294916
  1.5 1.0 %copy-start.2 = (f32[2,192,256]{2,1,0:T(8,128)S(1)}, f32[2,192,256]{2,1,0:T(8,128)}, u32[]{:S(2)}) copy-start(f32[2,192,256]{2,1,0:T(8,128)} %projector.1) | copy-start | bytes 1179652
  2.9 8.4 %collective-permute-start = (f32[320,128]{1,0:T(8,128)S(1)}, f32[320,128]{1,0:T(8,128)S(1)}, u32[]{:S(2)}, u32[]{:S(2)}) collective-permute-start(f32[320,128]{1,0:T(8,128)S(1)} %get-tuple-element.26), channel_id=1, source_target_pairs={{0,2},{2,4},{4,6},{6,0},{1,3},{3,5},{5,7},{7,1},{8,10},{10,12},{12... | collective-permute-start | bytes 491528 | tf_op jit(solution)/shard_map/ppermute | solution.py:255
  5.0 11.0 %collective-permute-start.1 = (f32[320,128]{1,0:T(8,128)S(1)}, f32[320,128]{1,0:T(8,128)S(1)}, u32[]{:S(2)}, u32[]{:S(2)}) collective-permute-start(f32[320,128]{1,0:T(8,128)S(1)} %get-tuple-element.27), channel_id=1, source_target_pairs={{0,4},{2,6},{4,0},{6,2},{1,5},{3,7},{5,1},{7,3},{8,12},{10,14},{12... | collective-permute-start | bytes 491528 | tf_op jit(solution)/shard_map/ppermute | solution.py:255
  8.6 7.4 %collective-permute-start.2 = (f32[320,128]{1,0:T(8,128)S(1)}, f32[320,128]{1,0:T(8,128)S(1)}, u32[]{:S(2)}, u32[]{:S(2)}) collective-permute-start(f32[320,128]{1,0:T(8,128)S(1)} %get-tuple-element.28), channel_id=1, source_target_pairs={{0,6},{2,0},{4,2},{6,4},{1,7},{3,1},{5,3},{7,5},{8,14},{10,8},{12,... | collective-permute-start | bytes 491528 | tf_op jit(solution)/shard_map/ppermute | solution.py:255
  32.3 14.5 %copy-start.1 = (bf16[2,192,128]{2,1,0:T(8,128)(2,1)S(1)}, bf16[2,192,128]{2,1,0:T(8,128)(2,1)}, u32[]{:S(2)}) copy-start(bf16[2,192,128]{2,1,0:T(8,128)(2,1)} %gradient.7) | copy-start | bytes 294916
  45.1 5.0 %copy-start.3 = (f32[2,64,128]{2,1,0:T(8,128)S(1)}, f32[2,64,128]{2,1,0:T(8,128)}, u32[]{:S(2)}) copy-start(f32[2,64,128]{2,1,0:T(8,128)} %first.3) | copy-start | bytes 196612
  45.1 5.0 %copy-start.4 = (f32[2,64,128]{2,1,0:T(8,128)S(1)}, f32[2,64,128]{2,1,0:T(8,128)}, u32[]{:S(2)}) copy-start(f32[2,64,128]{2,1,0:T(8,128)} %second.3) | copy-start | bytes 196612
  45.1 12.0 %collective-permute-start.3 = (f32[768,128]{1,0:T(8,128)S(1)}, f32[768,128]{1,0:T(8,128)S(1)}, u32[]{:S(2)}, u32[]{:S(2)}) collective-permute-start(f32[768,128]{1,0:T(8,128)S(1)} %bitcast.2), channel_id=1, source_target_pairs={{0,2},{2,0},{4,6},{6,4},{1,3},{3,1},{5,7},{7,5},{8,10},{10,8},{12,... | collective-permute-start | bytes 1179656 | tf_op jit(solution)/shard_map/ppermute | solution.py:258
  46.8 3.2 %copy-start.7 = (f32[2,192]{1,0:T(2,128)S(1)}, f32[2,192]{1,0:T(2,128)}, u32[]{:S(2)}) copy-start(f32[2,192]{1,0:T(2,128)} %gain_gradient.1) | copy-start | bytes 4612
  46.8 3.2 %copy-start.8 = (f32[2,192]{1,0:T(2,128)S(1)}, f32[2,192]{1,0:T(2,128)}, u32[]{:S(2)}) copy-start(f32[2,192]{1,0:T(2,128)} %gain_first.1) | copy-start | bytes 4612
  46.8 3.2 %copy-start.9 = (f32[2,192]{1,0:T(2,128)S(1)}, f32[2,192]{1,0:T(2,128)}, u32[]{:S(2)}) copy-start(f32[2,192]{1,0:T(2,128)} %gain_second.1) | copy-start | bytes 4612
  47.4 2.6 %copy-start.6 = (f32[2,192]{1,0:T(2,128)S(1)}, f32[2,192]{1,0:T(2,128)}, u32[]{:S(2)}) copy-start(f32[2,192]{1,0:T(2,128)} %gains.1) | copy-start | bytes 4612
  47.4 2.6 %copy-start.10 = (s32[2]{0:T(128)S(1)}, s32[2]{0:T(128)}, u32[]{:S(2)}) copy-start(s32[2]{0:T(128)} %steps.3) | copy-start | bytes 28
  47.4 21.0 %collective-permute-start.5 = (f32[448,128]{1,0:T(8,128)S(1)}, f32[448,128]{1,0:T(8,128)S(1)}, u32[]{:S(2)}, u32[]{:S(2)}) collective-permute-start(f32[448,128]{1,0:T(8,128)S(1)} %get-tuple-element.29.same), channel_id=1, source_target_pairs={{0,6},{2,4},{4,2},{6,0},{1,7},{3,5},{5,3},{7,1},{8,14},{10,12},{12... | collective-permute-start | bytes 688136 | tf_op jit(solution)/shard_map/ppermute | solution.py:258
  48.5 19.9 %collective-permute-start.4 = (f32[448,128]{1,0:T(8,128)S(1)}, f32[448,128]{1,0:T(8,128)S(1)}, u32[]{:S(2)}, u32[]{:S(2)}) collective-permute-start(f32[448,128]{1,0:T(8,128)S(1)} %get-tuple-element.34), channel_id=1, source_target_pairs={{0,4},{2,6},{4,0},{6,2},{1,5},{3,7},{5,1},{7,3},{8,12},{10,14},{12... | collective-permute-start | bytes 688136 | tf_op jit(solution)/shard_map/ppermute | solution.py:258
  51.3 11.9 %collective-permute-start.7 = (f32[256,128]{1,0:T(8,128)S(1)}, f32[256,128]{1,0:T(8,128)S(1)}, u32[]{:S(2)}, u32[]{:S(2)}) collective-permute-start(f32[256,128]{1,0:T(8,128)S(1)} %get-tuple-element.35), channel_id=1, source_target_pairs={{0,2},{2,4},{4,6},{6,0},{1,3},{3,5},{5,7},{7,1},{8,10},{10,12},{12... | collective-permute-start | bytes 393224 | tf_op jit(solution)/shard_map/ppermute | solution.py:255
  52.9 15.5 %collective-permute-start.8 = (f32[256,128]{1,0:T(8,128)S(1)}, f32[256,128]{1,0:T(8,128)S(1)}, u32[]{:S(2)}, u32[]{:S(2)}) collective-permute-start(f32[256,128]{1,0:T(8,128)S(1)} %get-tuple-element.35), channel_id=1, source_target_pairs={{0,4},{2,6},{4,0},{6,2},{1,5},{3,7},{5,1},{7,3},{8,12},{10,14},{12... | collective-permute-start | bytes 393224 | tf_op jit(solution)/shard_map/ppermute | solution.py:255
  57.0 11.4 %collective-permute-start.9 = (f32[256,128]{1,0:T(8,128)S(1)}, f32[256,128]{1,0:T(8,128)S(1)}, u32[]{:S(2)}, u32[]{:S(2)}) collective-permute-start(f32[256,128]{1,0:T(8,128)S(1)} %get-tuple-element.35), channel_id=1, source_target_pairs={{0,6},{2,0},{4,2},{6,4},{1,7},{3,1},{5,3},{7,5},{8,14},{10,8},{12,... | collective-permute-start | bytes 393224 | tf_op jit(solution)/shard_map/ppermute | solution.py:255
  63.2 5.5 %collective-permute-start.6 = (f32[128,128]{1,0:T(8,128)S(1)}, f32[128,128]{1,0:T(8,128)S(1)}, u32[]{:S(2)}, u32[]{:S(2)}) collective-permute-start(f32[128,128]{1,0:T(8,128)S(1)} %get-tuple-element.31.joint), channel_id=1, source_target_pairs={{0,6},{2,4},{4,2},{6,0},{1,7},{3,5},{5,3},{7,1},{8,14},{10,12},{12... | collective-permute-start | bytes 196616 | tf_op jit(solution)/shard_map/ppermute | solution.py:258
  65.1 3.6 %copy-start.5 = (bf16[2,192,128]{2,1,0:T(8,128)(2,1)S(1)}, bf16[2,192,128]{2,1,0:T(8,128)(2,1)}, u32[]{:S(2)}) copy-start(bf16[2,192,128]{2,1,0:T(8,128)(2,1)} %weight.1) | copy-start | bytes 294916
